TPU v7x, 32 devices: a whole 2x2x4 slice. The times are simulated.
32 devices in a mesh: grp: 1, ep: 32 (over z, y, x, core).
Axes of the slice: x: 2, y: 2, z: 4, core: 2. Of those that a mesh axis runs over, the one named last changes fastest.
Arguments:
- hidden_states: bfloat16 [192, 3584], P(('grp', 'ep')), may hold values from -6 to 6
- norm_gain: float32 [3584], replicated, may hold values from 0.1 to 1.9
- gate_scores: float32 [192, 8], P(('grp', 'ep')), may hold values from 0.05 to 1
- routes: int32 [192, 8], P(('grp', 'ep')), may hold values from 0 to 15, all different within a row; in each aligned block of 6 rows (0 to 5, 6 to 11, ...) at most 6 rows name the same one
- draft_counts: int32 [64], P(('grp', 'ep')), may hold values from 1 to 2
- w_gate: bfloat16 [32, 3584, 512], P('ep'), may hold values from -0.09375 to 0.09375
- w_up: bfloat16 [32, 3584, 512], P('ep'), may hold values from -0.09375 to 0.09375
- w_down: bfloat16 [32, 512, 3584], P('ep'), may hold values from -0.1875 to 0.1875
Outputs:
- moe_out: bfloat16 [192, 3584], P(('grp', 'ep'))
Inputs may be any that keep to these rules, and one draw needn't show every extreme that they name: `routes`: each token slot names 8 different experts; among the 6 token slots of one device no expert is named more than 6 times.
All inputs are finite; a program needn't handle non-finite values.
Results may differ from a plain program's by a relative error of at most 0.0077.
Values may be sent and summed in bfloat16 or wider, within the bound.
No kernel may reach another device: no remote copies, remote signals or barrier semaphores. Data moves between devices by JAX's collectives and lax.ppermute only.
A program may use at most 64 MiB of HBM per device.

v0:
```python
import math

import jax
import jax.numpy as jnp
from jax import lax
from jax.experimental import pallas as pl
from jax.experimental.pallas import tpu as pltpu
from jax.sharding import PartitionSpec as P


VMEM = pl.BlockSpec(memory_space=pltpu.VMEM)
ANY = pl.BlockSpec(memory_space=pl.ANY)
HBM = pl.BlockSpec(memory_space=pltpu.HBM)
PARTS = 4
MIB = 1024 * 1024


def swapped(array, *distances):
    size = lax.axis_size("ep")
    pairs = [(i, i ^ distances[i % len(distances)]) for i in range(size)]
    return lax.ppermute(array, "ep", pairs)


def core():
    return lax.rem(lax.axis_index("ep"), 2)


def ordered(own, other):
    first = core() == 0
    return jnp.where(first, own, other), jnp.where(first, other, own)


def wide(ref):
    return ref[...].astype(jnp.float32)


def lane_round(count):
    return -(-count // 128) * 128


def call(kernel, outs, limit, *args, specs=None, flops=0, scratch=()):
    moved = sum(math.prod(a.shape) * a.dtype.itemsize for a in (*args, *outs))
    single = len(outs) == 1
    return pl.pallas_call(
        kernel,
        out_shape=outs[0] if single else tuple(outs),
        in_specs=specs or [VMEM] * len(args),
        out_specs=VMEM if single else tuple([VMEM] * len(outs)),
        scratch_shapes=list(scratch),
        compiler_params=pltpu.CompilerParams(vmem_limit_bytes=limit),
        cost_estimate=pl.CostEstimate(flops=flops, bytes_accessed=moved, transcendentals=0),
    )(*args)


def pack_kernel(
    draft_hbm, states_hbm, gain_hbm, scores_hbm, routes_hbm, out_ref,
    draft_ref, states_ref, gain_ref, scores_ref, routes_ref, sems,
):
    sources = (draft_hbm, states_hbm, gain_hbm, scores_hbm, routes_hbm)
    targets = (draft_ref, states_ref, gain_ref, scores_ref, routes_ref)
    copies = [
        pltpu.make_async_copy(source, target, sems.at[i])
        for i, (source, target) in enumerate(zip(sources, targets))
    ]
    for copy in copies:
        copy.start()
    for copy in copies:
        copy.wait()
    tokens, width = states_ref.shape
    piece = width // PARTS
    extra = out_ref.shape[1] - piece
    requests = draft_ref.shape[0]
    slots = tokens // requests
    states = wide(states_ref)
    mean_square = jnp.mean(states * states, axis=-1, keepdims=True)
    normed = (states * lax.rsqrt(mean_square + 1e-06) * gain_ref[...].reshape(1, width)).astype(jnp.bfloat16)
    scores = scores_ref[...]
    weights = 2.5 * scores / jnp.sum(scores, axis=-1, keepdims=True)
    row = lax.broadcasted_iota(jnp.int32, (tokens, 1), 0)
    live = jnp.zeros((tokens, 1), jnp.bool_)
    for request in range(requests):
        inside = (row >= request * slots) & (row <= request * slots + draft_ref[request])
        live = live | (inside & (row < (request + 1) * slots))
    weights = jnp.where(live, weights, 0.0)
    lane = lax.broadcasted_iota(jnp.int32, (tokens, extra), 1)
    coefficient = jnp.zeros((tokens, extra), jnp.float32)
    for k in range(routes_ref.shape[1]):
        coefficient += jnp.where(routes_ref[:, k : k + 1] == lane, weights[:, k : k + 1], 0.0)
    coarse = coefficient.astype(jnp.bfloat16)
    fine = (coefficient - coarse.astype(jnp.float32)).astype(jnp.bfloat16)
    zero = jnp.zeros((tokens, extra), jnp.float32)
    coarse, fine = coarse.astype(jnp.float32), fine.astype(jnp.float32)
    sides = [coarse, fine] + [zero] * (PARTS - 2)
    normed = normed.astype(jnp.float32)
    normed = jnp.concatenate([normed[:, p * piece : (p + 1) * piece] for p in range(PARTS)], axis=0)
    rows = jnp.concatenate([normed, jnp.concatenate(sides, axis=0)], axis=1).astype(jnp.bfloat16)
    out_ref[...] = rows


def load_kernel(*refs):
    count = (len(refs) - 2) // 2
    token_ref, sems = refs[-2:]
    token_ref[...] = jnp.zeros_like(token_ref)
    copies = [
        pltpu.make_async_copy(refs[i], refs[count + i], sems.at[i]) for i in range(count)
    ]
    for copy in copies:
        copy.start()
    for copy in copies:
        copy.wait()


def combine_kernel(own_ref, beside_ref, far_ref, far_beside_ref, after_ref, out_ref, side_ref):
    tokens = own_ref.shape[0] // PARTS
    piece = own_ref.shape[1] - (PARTS * own_ref.shape[1] - out_ref.shape[1]) // 2

    def unfolded(rows):
        parts = [rows[p * tokens : (p + 1) * tokens] for p in range(PARTS)]
        columns = []
        for side in range(2):
            columns += [p[:, :piece] for p in parts[2 * side : 2 * side + 2]]
            columns.append(parts[side][:, piece:])
        return jnp.concatenate(columns, axis=1)

    blocks = ordered(wide(own_ref), wide(beside_ref)) + ordered(wide(far_ref), wide(far_beside_ref))
    rows = jnp.concatenate([unfolded(b) for b in blocks], axis=0)
    out_ref[...] = rows.astype(jnp.bfloat16)
    middle = rows.shape[1] // 2
    side_ref[...] = ordered(rows[:, :middle], rows[:, middle:])[0].astype(jnp.bfloat16)


def hidden_rows(lows, highs, gate_ref, up_ref):
    half = gate_ref.shape[1] // 2
    low, high = jnp.concatenate(lows, axis=0), jnp.concatenate(highs, axis=0)
    mixed = low[:, half:] + high[:, half:]
    lane = lax.broadcasted_iota(jnp.int32, mixed.shape, 1)
    expert = lax.axis_index("ep") // 2
    coefficient = jnp.sum(jnp.where(lane == expert, mixed, 0.0), axis=1, keepdims=True)
    low = low[:, :half].astype(jnp.bfloat16)
    high = high[:, :half].astype(jnp.bfloat16)

    def projected(ref):
        first = jnp.dot(low, ref[0, :half], preferred_element_type=jnp.float32)
        return first + jnp.dot(high, ref[0, half:], preferred_element_type=jnp.float32)

    gate = projected(gate_ref)
    up = projected(up_ref)
    return (gate / (1.0 + jnp.exp(-gate)) * up).astype(jnp.bfloat16), coefficient


def halves(ref):
    middle = ref.shape[1] // 2
    return ref[:, :middle].astype(jnp.float32), ref[:, middle:].astype(jnp.float32)


def lowered(hidden, coefficient, down_ref, first, count):
    columns = down_ref[0, :, first : first + count]
    return jnp.dot(hidden, columns, preferred_element_type=jnp.float32) * coefficient


def own_kernel(*refs):
    *refs, keep_ref, side_keep_ref, side_give_ref = refs
    block_ref, side_ref, side_beside_ref, *others, gate_ref, up_ref, down_ref = refs
    lows, highs = zip(*[halves(ref) for ref in (block_ref, *others)])
    side_low, side_high = ordered(wide(side_ref), wide(side_beside_ref))
    hidden, coefficient = hidden_rows(
        [*lows, side_low], [*highs, side_high], gate_ref, up_ref
    )
    rows, width = keep_ref.shape
    half = width // 2
    step = half // 2
    for start in range(0, half, step):
        low = lowered(hidden, coefficient, down_ref, start, step)
        high = lowered(hidden, coefficient, down_ref, half + start, step)
        keep_ref[:, start : start + step] = low[:rows]
        keep_ref[:, half + start : half + start + step] = high[:rows]
        keep, give = ordered(low[rows:], high[rows:])
        side_keep_ref[:, start : start + step] = keep
        side_give_ref[:, start : start + step] = give.astype(jnp.bfloat16)


def low_kernel(*refs):
    *others, gate_ref, up_ref, down_ref, after_ref, give_ref, hidden_ref, coefficient_ref = refs
    lows, highs = zip(*[halves(ref) for ref in others])
    hidden, coefficient = hidden_rows(lows, highs, gate_ref, up_ref)
    hidden_ref[...] = hidden
    coefficient_ref[...] = jnp.broadcast_to(coefficient, coefficient_ref.shape)
    half = give_ref.shape[1]
    step = half // 2
    for start in range(0, half, step):
        low = lowered(hidden, coefficient, down_ref, start, step)
        give_ref[:, start : start + step] = low.astype(jnp.bfloat16)


def high_kernel(hidden_ref, coefficient_ref, down_ref, give_ref):
    hidden, coefficient = hidden_ref[...], coefficient_ref[:, :1]
    half = give_ref.shape[1]
    step = half // 2
    for start in range(0, half, step):
        high = lowered(hidden, coefficient, down_ref, half + start, step)
        give_ref[:, start : start + step] = high.astype(jnp.bfloat16)


def fold_kernel(*refs):
    keep_ref, low_ref, high_ref, side_keep_ref, side_other_ref, *outs, side_out_ref = refs
    half = low_ref.shape[1]
    count = side_out_ref.shape[0]
    side_out_ref[...] = (side_keep_ref[...] + wide(side_other_ref)).astype(jnp.bfloat16)
    for j, out_ref in enumerate(outs):
        rows = slice(j * count, (j + 1) * count)
        kept = slice((j + 1) * count, (j + 2) * count)
        low = keep_ref[kept, :half] + low_ref[rows, :].astype(jnp.float32)
        high = keep_ref[kept, half:] + high_ref[rows, :].astype(jnp.float32)
        out_ref[:, :half] = low.astype(jnp.bfloat16)
        out_ref[:, half:] = high.astype(jnp.bfloat16)


def sum_kernel(*refs):
    keep_ref, side_ref, *parts, mine_ref, give_ref = refs
    rows, half = side_ref.shape
    tokens = rows // 4
    total = keep_ref[:rows, :]
    for ref in parts:
        total += wide(ref)
    side = wide(side_ref)
    zero = jnp.zeros_like(side)
    total += jnp.concatenate(ordered(side, zero), axis=1)
    near = ordered(total[:tokens], total[tokens : 2 * tokens])
    far = ordered(total[2 * tokens : 3 * tokens], total[3 * tokens :])

    def folded(which):
        columns = (slice(0, half), slice(half, 2 * half))
        return jnp.concatenate([b[which][:, c] for c in columns for b in (near, far)], axis=0)

    mine_ref[...] = folded(0)
    give_ref[...] = folded(1).astype(jnp.bfloat16)


def split_kernel(mine_ref, other_ref, near_ref, far_ref):
    total = mine_ref[...] + wide(other_ref)
    tokens = total.shape[0] // 4
    piece = near_ref.shape[1]

    def folded(which):
        pieces = []
        for side in range(2):
            start = (2 * side + which) * tokens
            rows = total[start : start + tokens]
            pieces += [rows[:, :piece], rows[:, piece:]]
        return jnp.concatenate(pieces, axis=0)

    near_ref[...] = folded(0)
    far_ref[...] = folded(1).astype(jnp.bfloat16)


def finish_kernel(near_ref, other_ref, out_ref):
    tokens, width = out_ref.shape
    piece = width // PARTS
    total = near_ref[...] + wide(other_ref)
    for p in range(PARTS):
        rows = total[p * tokens : (p + 1) * tokens]
        out_ref[:, p * piece : (p + 1) * piece] = rows.astype(jnp.bfloat16)


def body(hidden_states, norm_gain, gate_scores, routes, draft_counts, w_gate, w_up, w_down):
    tokens, width = hidden_states.shape
    devices = lax.axis_size("ep")
    far = devices // 2
    shared = far - 2
    steps = [(hop, shared ^ hop) for hop in range(2, far // 2, 2)]
    half, piece = width // 2, width // PARTS
    extra = lane_round(far)
    shape = jax.ShapeDtypeStruct
    bf16, f32 = jnp.bfloat16, jnp.float32
    inner = w_gate.shape[2]

    small = [
        pltpu.with_memory_space_constraint(a, pltpu.HBM)
        for a in (draft_counts, hidden_states, norm_gain, gate_scores, routes)
    ]
    packed = call(
        pack_kernel,
        [shape((PARTS * tokens, piece + extra), bf16)],
        4 * MIB,
        *small,
        specs=[HBM] * 5,
        scratch=[pltpu.SMEM(draft_counts.shape, jnp.int32)]
        + [pltpu.VMEM(a.shape, a.dtype) for a in small[1:]]
        + [pltpu.SemaphoreType.DMA((5,))],
    )
    moved = swapped(packed, far)
    beside = swapped(packed, 1)
    weights = [pltpu.with_memory_space_constraint(w, pltpu.HBM) for w in (w_gate, w_up, w_down)]
    gate, up, token = call(
        load_kernel,
        [pltpu.VMEM(w.shape, w.dtype) for w in weights[:2]] + [shape((8, 128), f32)],
        MIB,
        *weights[:2],
        specs=[HBM] * 2,
        scratch=[pltpu.SemaphoreType.DMA((2,))],
    )
    gate, up = [pltpu.with_memory_space_constraint(w, pltpu.VMEM) for w in (gate, up)]
    rows = 4 * tokens
    block, side = call(
        combine_kernel,
        [shape((rows, width + 2 * extra), bf16), shape((rows, half + extra), bf16)],
        4 * MIB,
        packed,
        beside,
        moved,
        swapped(moved, 1),
        token,
        specs=[VMEM] * 4 + [ANY],
    )
    side = swapped(side, shared)
    parts = [swapped(block, *step) for step in steps]
    side_beside = swapped(side, 1)
    beside = [swapped(part, 1) for part in parts]
    count = len(steps)
    work = 2 * rows * width * inner
    down, token = call(
        load_kernel,
        [pltpu.VMEM(w_down.shape, w_down.dtype), shape((8, 128), f32)],
        MIB,
        weights[2],
        specs=[HBM],
        scratch=[pltpu.SemaphoreType.DMA((1,))],
    )
    down = pltpu.with_memory_space_constraint(down, pltpu.VMEM)
    keep, side_keep, side_give = call(
        own_kernel,
        [
            shape(((1 + count) * rows, width), f32),
            shape((rows, half), f32),
            shape((rows, half), bf16),
        ],
        16 * MIB,
        block,
        side,
        side_beside,
        *parts,
        gate,
        up,
        down,
        flops=3 * (2 + count) * work,
    )
    side_give = swapped(side_give, 1)
    low, hidden, coefficient = call(
        low_kernel,
        [
            shape((count * rows, half), bf16),
            shape((count * rows, inner), bf16),
            shape((count * rows, 128), f32),
        ],
        16 * MIB,
        *beside,
        gate,
        up,
        down,
        keep,
        specs=[VMEM] * (3 + count) + [ANY],
        flops=5 * count * work // 2,
    )
    low = swapped(low, 1)
    high = call(
        high_kernel,
        [shape((count * rows, half), bf16)],
        8 * MIB,
        hidden,
        coefficient,
        down,
        flops=count * work // 2,
    )
    high = swapped(high, 1)
    *parts, side = call(
        fold_kernel,
        [shape((rows, width), bf16)] * count + [shape((rows, half), bf16)],
        8 * MIB,
        keep,
        low,
        high,
        side_keep,
        side_give,
    )
    side = swapped(side, shared)
    parts = [swapped(part, *step) for part, step in zip(parts, steps)]
    mine, give = call(
        sum_kernel,
        [shape((rows, half), f32), shape((rows, half), bf16)],
        8 * MIB,
        keep,
        side,
        *parts,
    )
    near, give = call(
        split_kernel,
        [shape((PARTS * tokens, piece), f32), shape((PARTS * tokens, piece), bf16)],
        4 * MIB,
        mine,
        swapped(give, 1),
    )
    return call(finish_kernel, [shape((tokens, width), bf16)], 4 * MIB, near, swapped(give, far))


def solution(mesh):
    return jax.shard_map(
        body,
        mesh=mesh,
        in_specs=(
            P(("grp", "ep"), None),
            P(),
            P(("grp", "ep"), None),
            P(("grp", "ep"), None),
            P(("grp", "ep")),
            P("ep", None, None),
            P("ep", None, None),
            P("ep", None, None),
        ),
        out_specs=P(("grp", "ep"), None),
        check_vma=False,
    )
```

profile of v0, /device:TPU:0, one launch (start us, length us, event | category | flops | bytes accessed | tf_op | source)
XLA Modules:
  0.0 53.4 jit_solution(9368160853903174191)
XLA Ops:
  0.0 1.1 %shard_map.82.own_ref = bf16[24,1024]{1,0:T(8,128)(2,1)S(1)} custom-call(s32[2]{0:T(128)} %draft_hbm.1, bf16[6,3584]{1,0:T(8,128)(2,1)} %states_hbm.1, f32[3584]{0:T(1024)} %gain_hbm.1, f32[6,8]{1,0:T(8,128)} %scores_hbm.1, s32[6,8]{1,0:T(8,128)} %routes_hbm.1), custom_call_target="tpu_custom_call" | custom-call | bytes 106888 | tf_op jit(solution)/shard_map/pallas_call | solution.py:44
  1.1 4.1 %collective-permute-start.1 = (bf16[24,1024]{1,0:T(8,128)(2,1)S(1)}, bf16[24,1024]{1,0:T(8,128)(2,1)S(1)}, u32[]{:S(2)}, u32[]{:S(2)}) collective-permute-start(bf16[24,1024]{1,0:T(8,128)(2,1)S(1)} %shard_map.82.own_ref), channel_id=1, source_target_pairs={{0,16},{1,17},{2,18},{3,19},{4,20},{5,21},{6,22},{7,23},{8,24},{9,... | collective-permute-start | bytes 147464 | tf_op jit(solution)/shard_map/ppermute | solution.py:21
  5.2 2.6 %collective-permute-done.1.far_ref = bf16[24,1024]{1,0:T(8,128)(2,1)S(1)} collective-permute-done((bf16[24,1024]{1,0:T(8,128)(2,1)S(1)}, bf16[24,1024]{1,0:T(8,128)(2,1)S(1)}, u32[]{:S(2)}, u32[]{:S(2)}) %collective-permute-start.1) | collective-permute-done | bytes 49184 | tf_op jit(solution)/shard_map/ppermute | solution.py:21
  7.8 3.2 %shard_map.83 = (bf16[1,3584,512]{2,1,0:T(8,128)(2,1)S(1)}, bf16[1,3584,512]{2,1,0:T(8,128)(2,1)S(1)}, f32[8,128]{1,0:T(8,128)S(1)}) custom-call(bf16[1,3584,512]{2,1,0:T(8,128)(2,1)} %refs_0_.2, bf16[1,3584,512]{2,1,0:T(8,128)(2,1)} %refs_1_.1), custom_call_target="tpu_custom_call" | custom-call | bytes 14684160 | tf_op jit(solution)/shard_map/pallas_call | solution.py:44
  11.1 2.7 %collective-permute-start.7 = (bf16[24,3840]{1,0:T(8,128)(2,1)S(1)}, bf16[24,3840]{1,0:T(8,128)(2,1)S(1)}, u32[]{:S(2)}, u32[]{:S(2)}) collective-permute-start(bf16[24,3840]{1,0:T(8,128)(2,1)S(1)} %get-tuple-element.26.refs_0_), channel_id=1, source_target_pairs={{0,6},{1,9},{2,4},{3,11},{4,2},{5,13},{6,0},{7,15},{8,14},{9,1},{1... | collective-permute-start | bytes 552968 | tf_op jit(solution)/shard_map/ppermute | solution.py:21
  13.8 0.5 %collective-permute-start.5 = (bf16[24,3840]{1,0:T(8,128)(2,1)S(1)}, bf16[24,3840]{1,0:T(8,128)(2,1)S(1)}, u32[]{:S(2)}, u32[]{:S(2)}) collective-permute-start(bf16[24,3840]{1,0:T(8,128)(2,1)S(1)} %get-tuple-element.26.refs_0_), channel_id=1, source_target_pairs={{0,2},{1,13},{2,0},{3,15},{4,6},{5,9},{6,4},{7,11},{8,10},{9,5},{1... | collective-permute-start | bytes 552968 | tf_op jit(solution)/shard_map/ppermute | solution.py:21
  14.7 3.3 %collective-permute-start.3 = (bf16[24,1920]{1,0:T(8,128)(2,1)S(1)}, bf16[24,1920]{1,0:T(8,128)(2,1)S(1)}, u32[]{:S(2)}, u32[]{:S(2)}) collective-permute-start(bf16[24,1920]{1,0:T(8,128)(2,1)S(1)} %get-tuple-element.27), channel_id=1, source_target_pairs={{0,14},{1,15},{2,12},{3,13},{4,10},{5,11},{6,8},{7,9},{8,6},{9,7},... | collective-permute-start | bytes 276488 | tf_op jit(solution)/shard_map/ppermute | solution.py:21
  17.9 4.1 %collective-permute-done.3.refs_1_ = bf16[24,1920]{1,0:T(8,128)(2,1)S(1)} collective-permute-done((bf16[24,1920]{1,0:T(8,128)(2,1)S(1)}, bf16[24,1920]{1,0:T(8,128)(2,1)S(1)}, u32[]{:S(2)}, u32[]{:S(2)}) %collective-permute-start.3) | collective-permute-done | bytes 92192 | tf_op jit(solution)/shard_map/ppermute | solution.py:21
  22.0 2.4 %collective-permute-start.4 = (bf16[24,1920]{1,0:T(8,128)(2,1)S(1)}, bf16[24,1920]{1,0:T(8,128)(2,1)S(1)}, u32[]{:S(2)}, u32[]{:S(2)}) collective-permute-start(bf16[24,1920]{1,0:T(8,128)(2,1)S(1)} %collective-permute-done.3.refs_1_), channel_id=1, source_target_pairs={{0,1},{1,0},{2,3},{3,2},{4,5},{5,4},{6,7},{7,6},{8,9},{9,8},{10,11... | collective-permute-start | bytes 276488 | tf_op jit(solution)/shard_map/ppermute | solution.py:21
  25.1 2.6 %shard_map.85 = (bf16[1,512,3584]{2,1,0:T(8,128)(2,1)S(1)}, f32[8,128]{1,0:T(8,128)}) custom-call(bf16[1,512,3584]{2,1,0:T(8,128)(2,1)} %refs_0_.3), custom_call_target="tpu_custom_call" | custom-call | bytes 7344128 | tf_op jit(solution)/shard_map/pallas_call | solution.py:44
  27.7 1.8 %shard_map.86 = (f32[96,3584]{1,0:T(8,128)S(1)}, f32[24,1792]{1,0:T(8,128)S(1)}, bf16[24,1792]{1,0:T(8,128)(2,1)S(1)}) custom-call(bf16[24,3840]{1,0:T(8,128)(2,1)S(1)} %get-tuple-element.26.refs_0_, bf16[24,1920]{1,0:T(8,128)(2,1)S(1)} %collective-permute-done.3.refs_1_, bf16[24,1920]{1,0:T(8,128)(2,1)S(1)} %collective-permute-done.4.refs_2_, ...), custom_call_target="tpu_custom_call" | custom-call | flops 1321205760 | bytes 13565952 | tf_op jit(solution)/shard_map/pallas_call | solution.py:44
  29.6 1.8 %shard_map.87 = (bf16[72,1792]{1,0:T(8,128)(2,1)S(1)}, bf16[72,512]{1,0:T(8,128)(2,1)S(1)}, f32[72,128]{1,0:T(8,128)S(1)}) custom-call(bf16[24,3840]{1,0:T(8,128)(2,1)S(1)} %collective-permute-done.8.refs_0_, bf16[24,3840]{1,0:T(8,128)(2,1)S(1)} %collective-permute-done.9.refs_1_, bf16[24,3840]{1,0:T(8,128)(2,1)S(1)} %collective-permute-done.10.refs_2_, ...), custom_call_target="tpu_custom_call" | custom-call | flops 660602880 | bytes 13307904 | tf_op jit(solution)/shard_map/pallas_call | solution.py:44
  31.8 0.5 collective-permute-start.12
  32.8 1.1 %collective-permute-done.13.refs_4_ = bf16[24,1792]{1,0:T(8,128)(2,1)S(1)} collective-permute-done((bf16[24,1792]{1,0:T(8,128)(2,1)S(1)}, bf16[24,1792]{1,0:T(8,128)(2,1)S(1)}, u32[]{:S(2)}, u32[]{:S(2)}) %collective-permute-start.13) | collective-permute-done | bytes 86048 | tf_op jit(solution)/shard_map/ppermute | solution.py:21
  34.1 1.2 %collective-permute-start.15 = (bf16[24,3584]{1,0:T(8,128)(2,1)S(1)}, bf16[24,3584]{1,0:T(8,128)(2,1)S(1)}, u32[]{:S(2)}, u32[]{:S(2)}) collective-permute-start(bf16[24,3584]{1,0:T(8,128)(2,1)S(1)} %get-tuple-element.38), channel_id=1, source_target_pairs={{0,2},{1,13},{2,0},{3,15},{4,6},{5,9},{6,4},{7,11},{8,10},{9,5},{1... | collective-permute-start | bytes 516104 | tf_op jit(solution)/shard_map/ppermute | solution.py:21
  35.3 0.6 %collective-permute-start.16 = (bf16[24,3584]{1,0:T(8,128)(2,1)S(1)}, bf16[24,3584]{1,0:T(8,128)(2,1)S(1)}, u32[]{:S(2)}, u32[]{:S(2)}) collective-permute-start(bf16[24,3584]{1,0:T(8,128)(2,1)S(1)} %get-tuple-element.39), channel_id=1, source_target_pairs={{0,4},{1,11},{2,6},{3,9},{4,0},{5,15},{6,2},{7,13},{8,12},{9,3},{1... | collective-permute-start | bytes 516104 | tf_op jit(solution)/shard_map/ppermute | solution.py:21
  35.9 1.7 %collective-permute-start.17 = (bf16[24,3584]{1,0:T(8,128)(2,1)S(1)}, bf16[24,3584]{1,0:T(8,128)(2,1)S(1)}, u32[]{:S(2)}, u32[]{:S(2)}) collective-permute-start(bf16[24,3584]{1,0:T(8,128)(2,1)S(1)} %get-tuple-element.40), channel_id=1, source_target_pairs={{0,6},{1,9},{2,4},{3,11},{4,2},{5,13},{6,0},{7,15},{8,14},{9,1},{1... | collective-permute-start | bytes 516104 | tf_op jit(solution)/shard_map/ppermute | solution.py:21
  37.6 1.9 %collective-permute-start.14 = (bf16[24,1792]{1,0:T(8,128)(2,1)S(1)}, bf16[24,1792]{1,0:T(8,128)(2,1)S(1)}, u32[]{:S(2)}, u32[]{:S(2)}) collective-permute-start(bf16[24,1792]{1,0:T(8,128)(2,1)S(1)} %get-tuple-element.37), channel_id=1, source_target_pairs={{0,14},{1,15},{2,12},{3,13},{4,10},{5,11},{6,8},{7,9},{8,6},{9,7},... | collective-permute-start | bytes 258056 | tf_op jit(solution)/shard_map/ppermute | solution.py:21
  39.5 5.3 %collective-permute-done.14.refs_1_ = bf16[24,1792]{1,0:T(8,128)(2,1)S(1)} collective-permute-done((bf16[24,1792]{1,0:T(8,128)(2,1)S(1)}, bf16[24,1792]{1,0:T(8,128)(2,1)S(1)}, u32[]{:S(2)}, u32[]{:S(2)}) %collective-permute-start.14) | collective-permute-done | bytes 86048 | tf_op jit(solution)/shard_map/ppermute | solution.py:21
  45.0 0.8 %collective-permute-start.18 = (bf16[24,1792]{1,0:T(8,128)(2,1)S(1)}, bf16[24,1792]{1,0:T(8,128)(2,1)S(1)}, u32[]{:S(2)}, u32[]{:S(2)}) collective-permute-start(bf16[24,1792]{1,0:T(8,128)(2,1)S(1)} %get-tuple-element.42), channel_id=1, source_target_pairs={{0,1},{1,0},{2,3},{3,2},{4,5},{5,4},{6,7},{7,6},{8,9},{9,8},{10,11... | collective-permute-start | bytes 258056 | tf_op jit(solution)/shard_map/ppermute | solution.py:21
  45.9 0.9 %collective-permute-done.18.other_ref = bf16[24,1792]{1,0:T(8,128)(2,1)S(1)} collective-permute-done((bf16[24,1792]{1,0:T(8,128)(2,1)S(1)}, bf16[24,1792]{1,0:T(8,128)(2,1)S(1)}, u32[]{:S(2)}, u32[]{:S(2)}) %collective-permute-start.18) | collective-permute-done | bytes 86048 | tf_op jit(solution)/shard_map/ppermute | solution.py:21
  46.8 2.7 %collective-permute-start.19 = (bf16[24,896]{1,0:T(8,128)(2,1)S(1)}, bf16[24,896]{1,0:T(8,128)(2,1)S(1)}, u32[]{:S(2)}, u32[]{:S(2)}) collective-permute-start(bf16[24,896]{1,0:T(8,128)(2,1)S(1)} %get-tuple-element.44), channel_id=1, source_target_pairs={{0,16},{1,17},{2,18},{3,19},{4,20},{5,21},{6,22},{7,23},{8,24},{9,... | collective-permute-start | bytes 129032 | tf_op jit(solution)/shard_map/ppermute | solution.py:21
  49.5 3.2 %collective-permute-done.19.other_ref = bf16[24,896]{1,0:T(8,128)(2,1)S(1)} collective-permute-done((bf16[24,896]{1,0:T(8,128)(2,1)S(1)}, bf16[24,896]{1,0:T(8,128)(2,1)S(1)}, u32[]{:S(2)}, u32[]{:S(2)}) %collective-permute-start.19) | collective-permute-done | bytes 43040 | tf_op jit(solution)/shard_map/ppermute | solution.py:21
  52.8 0.6 %shard_map.92 = bf16[6,3584]{1,0:T(8,128)(2,1)} custom-call(f32[24,896]{1,0:T(8,128)S(1)} %get-tuple-element.43.near_ref, bf16[24,896]{1,0:T(8,128)(2,1)S(1)} %collective-permute-done.19.other_ref), custom_call_target="tpu_custom_call" | custom-call | bytes 172032 | tf_op jit(solution)/shard_map/pallas_call | solution.py:44
  (27 shorter events, 2.3 us)
Async XLA Ops:
  1.1 6.7 %collective-permute-start.1 = (bf16[24,1024]{1,0:T(8,128)(2,1)S(1)}, bf16[24,1024]{1,0:T(8,128)(2,1)S(1)}, u32[]{:S(2)}, u32[]{:S(2)}) collective-permute-start(bf16[24,1024]{1,0:T(8,128)(2,1)S(1)} %shard_map.82.own_ref), channel_id=1, source_target_pairs={{0,16},{1,17},{2,18},{3,19},{4,20},{5,21},{6,22},{7,23},{8,24},{9,... | collective-permute-start | bytes 147464 | tf_op jit(solution)/shard_map/ppermute | solution.py:21
  5.2 5.8 %collective-permute-start = (bf16[24,1024]{1,0:T(8,128)(2,1)S(1)}, bf16[24,1024]{1,0:T(8,128)(2,1)S(1)}, u32[]{:S(2)}, u32[]{:S(2)}) collective-permute-start(bf16[24,1024]{1,0:T(8,128)(2,1)S(1)} %shard_map.82.own_ref), channel_id=1, source_target_pairs={{0,1},{1,0},{2,3},{3,2},{4,5},{5,4},{6,7},{7,6},{8,9},{9,8},{10,11... | collective-permute-start | bytes 147464 | tf_op jit(solution)/shard_map/ppermute | solution.py:21
  7.8 3.2 %collective-permute-start.2 = (bf16[24,1024]{1,0:T(8,128)(2,1)S(1)}, bf16[24,1024]{1,0:T(8,128)(2,1)S(1)}, u32[]{:S(2)}, u32[]{:S(2)}) collective-permute-start(bf16[24,1024]{1,0:T(8,128)(2,1)S(1)} %collective-permute-done.1.far_ref), channel_id=1, source_target_pairs={{0,1},{1,0},{2,3},{3,2},{4,5},{5,4},{6,7},{7,6},{8,9},{9,8},{10,11... | collective-permute-start | bytes 147464 | tf_op jit(solution)/shard_map/ppermute | solution.py:21
  11.1 13.3 %collective-permute-start.7 = (bf16[24,3840]{1,0:T(8,128)(2,1)S(1)}, bf16[24,3840]{1,0:T(8,128)(2,1)S(1)}, u32[]{:S(2)}, u32[]{:S(2)}) collective-permute-start(bf16[24,3840]{1,0:T(8,128)(2,1)S(1)} %get-tuple-element.26.refs_0_), channel_id=1, source_target_pairs={{0,6},{1,9},{2,4},{3,11},{4,2},{5,13},{6,0},{7,15},{8,14},{9,1},{1... | collective-permute-start | bytes 552968 | tf_op jit(solution)/shard_map/ppermute | solution.py:21
  13.8 10.6 %collective-permute-start.5 = (bf16[24,3840]{1,0:T(8,128)(2,1)S(1)}, bf16[24,3840]{1,0:T(8,128)(2,1)S(1)}, u32[]{:S(2)}, u32[]{:S(2)}) collective-permute-start(bf16[24,3840]{1,0:T(8,128)(2,1)S(1)} %get-tuple-element.26.refs_0_), channel_id=1, source_target_pairs={{0,2},{1,13},{2,0},{3,15},{4,6},{5,9},{6,4},{7,11},{8,10},{9,5},{1... | collective-permute-start | bytes 552968 | tf_op jit(solution)/shard_map/ppermute | solution.py:21
  14.4 10.6 %collective-permute-start.6 = (bf16[24,3840]{1,0:T(8,128)(2,1)S(1)}, bf16[24,3840]{1,0:T(8,128)(2,1)S(1)}, u32[]{:S(2)}, u32[]{:S(2)}) collective-permute-start(bf16[24,3840]{1,0:T(8,128)(2,1)S(1)} %get-tuple-element.26.refs_0_), channel_id=1, source_target_pairs={{0,4},{1,11},{2,6},{3,9},{4,0},{5,15},{6,2},{7,13},{8,12},{9,3},{1... | collective-permute-start | bytes 552968 | tf_op jit(solution)/shard_map/ppermute | solution.py:21
  14.7 7.3 %collective-permute-start.3 = (bf16[24,1920]{1,0:T(8,128)(2,1)S(1)}, bf16[24,1920]{1,0:T(8,128)(2,1)S(1)}, u32[]{:S(2)}, u32[]{:S(2)}) collective-permute-start(bf16[24,1920]{1,0:T(8,128)(2,1)S(1)} %get-tuple-element.27), channel_id=1, source_target_pairs={{0,14},{1,15},{2,12},{3,13},{4,10},{5,11},{6,8},{7,9},{8,6},{9,7},... | collective-permute-start | bytes 276488 | tf_op jit(solution)/shard_map/ppermute | solution.py:21
  22.0 5.7 %collective-permute-start.4 = (bf16[24,1920]{1,0:T(8,128)(2,1)S(1)}, bf16[24,1920]{1,0:T(8,128)(2,1)S(1)}, u32[]{:S(2)}, u32[]{:S(2)}) collective-permute-start(bf16[24,1920]{1,0:T(8,128)(2,1)S(1)} %collective-permute-done.3.refs_1_), channel_id=1, source_target_pairs={{0,1},{1,0},{2,3},{3,2},{4,5},{5,4},{6,7},{7,6},{8,9},{9,8},{10,11... | collective-permute-start | bytes 276488 | tf_op jit(solution)/shard_map/ppermute | solution.py:21
  24.5 5.1 %collective-permute-start.10 = (bf16[24,3840]{1,0:T(8,128)(2,1)S(1)}, bf16[24,3840]{1,0:T(8,128)(2,1)S(1)}, u32[]{:S(2)}, u32[]{:S(2)}) collective-permute-start(bf16[24,3840]{1,0:T(8,128)(2,1)S(1)} %collective-permute-done.7.refs_5_), channel_id=1, source_target_pairs={{0,1},{1,0},{2,3},{3,2},{4,5},{5,4},{6,7},{7,6},{8,9},{9,8},{10,11... | collective-permute-start | bytes 552968 | tf_op jit(solution)/shard_map/ppermute | solution.py:21
  24.5 5.1 %collective-permute-start.8 = (bf16[24,3840]{1,0:T(8,128)(2,1)S(1)}, bf16[24,3840]{1,0:T(8,128)(2,1)S(1)}, u32[]{:S(2)}, u32[]{:S(2)}) collective-permute-start(bf16[24,3840]{1,0:T(8,128)(2,1)S(1)} %collective-permute-done.5.refs_3_), channel_id=1, source_target_pairs={{0,1},{1,0},{2,3},{3,2},{4,5},{5,4},{6,7},{7,6},{8,9},{9,8},{10,11... | collective-permute-start | bytes 552968 | tf_op jit(solution)/shard_map/ppermute | solution.py:21
  25.0 4.6 %collective-permute-start.9 = (bf16[24,3840]{1,0:T(8,128)(2,1)S(1)}, bf16[24,3840]{1,0:T(8,128)(2,1)S(1)}, u32[]{:S(2)}, u32[]{:S(2)}) collective-permute-start(bf16[24,3840]{1,0:T(8,128)(2,1)S(1)} %collective-permute-done.6.refs_4_), channel_id=1, source_target_pairs={{0,1},{1,0},{2,3},{3,2},{4,5},{5,4},{6,7},{7,6},{8,9},{9,8},{10,11... | collective-permute-start | bytes 552968 | tf_op jit(solution)/shard_map/ppermute | solution.py:21
  31.8 2.2 %collective-permute-start.12 = (bf16[72,1792]{1,0:T(8,128)(2,1)S(1)}, bf16[72,1792]{1,0:T(8,128)(2,1)S(1)}, u32[]{:S(2)}, u32[]{:S(2)}) collective-permute-start(bf16[72,1792]{1,0:T(8,128)(2,1)S(1)} %shard_map.88), channel_id=1, source_target_pairs={{0,1},{1,0},{2,3},{3,2},{4,5},{5,4},{6,7},{7,6},{8,9},{9,8},{10,11... | collective-permute-start | bytes 774152 | tf_op jit(solution)/shard_map/ppermute | solution.py:21
  32.3 1.7 %collective-permute-start.11 = (bf16[72,1792]{1,0:T(8,128)(2,1)S(1)}, bf16[72,1792]{1,0:T(8,128)(2,1)S(1)}, u32[]{:S(2)}, u32[]{:S(2)}) collective-permute-start(bf16[72,1792]{1,0:T(8,128)(2,1)S(1)} %get-tuple-element.32), channel_id=1, source_target_pairs={{0,1},{1,0},{2,3},{3,2},{4,5},{5,4},{6,7},{7,6},{8,9},{9,8},{10,11... | collective-permute-start | bytes 774152 | tf_op jit(solution)/shard_map/ppermute | solution.py:21
  32.4 1.6 %collective-permute-start.13 = (bf16[24,1792]{1,0:T(8,128)(2,1)S(1)}, bf16[24,1792]{1,0:T(8,128)(2,1)S(1)}, u32[]{:S(2)}, u32[]{:S(2)}) collective-permute-start(bf16[24,1792]{1,0:T(8,128)(2,1)S(1)} %get-tuple-element.36), channel_id=1, source_target_pairs={{0,1},{1,0},{2,3},{3,2},{4,5},{5,4},{6,7},{7,6},{8,9},{9,8},{10,11... | collective-permute-start | bytes 258056 | tf_op jit(solution)/shard_map/ppermute | solution.py:21
  34.1 10.8 %collective-permute-start.15 = (bf16[24,3584]{1,0:T(8,128)(2,1)S(1)}, bf16[24,3584]{1,0:T(8,128)(2,1)S(1)}, u32[]{:S(2)}, u32[]{:S(2)}) collective-permute-start(bf16[24,3584]{1,0:T(8,128)(2,1)S(1)} %get-tuple-element.38), channel_id=1, source_target_pairs={{0,2},{1,13},{2,0},{3,15},{4,6},{5,9},{6,4},{7,11},{8,10},{9,5},{1... | collective-permute-start | bytes 516104 | tf_op jit(solution)/shard_map/ppermute | solution.py:21
  35.3 9.5 %collective-permute-start.16 = (bf16[24,3584]{1,0:T(8,128)(2,1)S(1)}, bf16[24,3584]{1,0:T(8,128)(2,1)S(1)}, u32[]{:S(2)}, u32[]{:S(2)}) collective-permute-start(bf16[24,3584]{1,0:T(8,128)(2,1)S(1)} %get-tuple-element.39), channel_id=1, source_target_pairs={{0,4},{1,11},{2,6},{3,9},{4,0},{5,15},{6,2},{7,13},{8,12},{9,3},{1... | collective-permute-start | bytes 516104 | tf_op jit(solution)/shard_map/ppermute | solution.py:21
  35.9 8.9 %collective-permute-start.17 = (bf16[24,3584]{1,0:T(8,128)(2,1)S(1)}, bf16[24,3584]{1,0:T(8,128)(2,1)S(1)}, u32[]{:S(2)}, u32[]{:S(2)}) collective-permute-start(bf16[24,3584]{1,0:T(8,128)(2,1)S(1)} %get-tuple-element.40), channel_id=1, source_target_pairs={{0,6},{1,9},{2,4},{3,11},{4,2},{5,13},{6,0},{7,15},{8,14},{9,1},{1... | collective-permute-start | bytes 516104 | tf_op jit(solution)/shard_map/ppermute | solution.py:21
  37.6 7.2 %collective-permute-start.14 = (bf16[24,1792]{1,0:T(8,128)(2,1)S(1)}, bf16[24,1792]{1,0:T(8,128)(2,1)S(1)}, u32[]{:S(2)}, u32[]{:S(2)}) collective-permute-start(bf16[24,1792]{1,0:T(8,128)(2,1)S(1)} %get-tuple-element.37), channel_id=1, source_target_pairs={{0,14},{1,15},{2,12},{3,13},{4,10},{5,11},{6,8},{7,9},{8,6},{9,7},... | collective-permute-start | bytes 258056 | tf_op jit(solution)/shard_map/ppermute | solution.py:21
  45.0 1.8 %collective-permute-start.18 = (bf16[24,1792]{1,0:T(8,128)(2,1)S(1)}, bf16[24,1792]{1,0:T(8,128)(2,1)S(1)}, u32[]{:S(2)}, u32[]{:S(2)}) collective-permute-start(bf16[24,1792]{1,0:T(8,128)(2,1)S(1)} %get-tuple-element.42), channel_id=1, source_target_pairs={{0,1},{1,0},{2,3},{3,2},{4,5},{5,4},{6,7},{7,6},{8,9},{9,8},{10,11... | collective-permute-start | bytes 258056 | tf_op jit(solution)/shard_map/ppermute | solution.py:21
  46.8 5.9 %collective-permute-start.19 = (bf16[24,896]{1,0:T(8,128)(2,1)S(1)}, bf16[24,896]{1,0:T(8,128)(2,1)S(1)}, u32[]{:S(2)}, u32[]{:S(2)}) collective-permute-start(bf16[24,896]{1,0:T(8,128)(2,1)S(1)} %get-tuple-element.44), channel_id=1, source_target_pairs={{0,16},{1,17},{2,18},{3,19},{4,20},{5,21},{6,22},{7,23},{8,24},{9,... | collective-permute-start | bytes 129032 | tf_op jit(solution)/shard_map/ppermute | solution.py:21
where the time goes:
time: 53.6 us; the launch traced here: 53.4 us
  starting transfers between devices  23.9 us (45%)
  waiting for transfers between devices  17.3 us (32%)
  Pallas kernels  12 us (22%)
    ppermute x20, starting transfers between devices, swapped(): return lax.ppermute(array, 'ep', pairs)  23.9 us
    ppermute x20, waiting for transfers between devices, swapped(): return lax.ppermute(array, 'ep', pairs)  17.3 us
    pallas_call x11, Pallas kernels, call(): pl.pallas_call(kernel, out_shape=outs[0] if single else tuple(outs), in_s...  12 us
  transfers between devices with their start and end apart: 20, of which 6 were waited for; matrix products, arithmetic and copies ran while one was open for 0% of the time, Pallas kernels for 14%

commit v1 on v0

--- a/solution.py
+++ b/solution.py
@@ -158,59 +158,77 @@
     return jnp.dot(hidden, columns, preferred_element_type=jnp.float32) * coefficient
 
 
-def own_kernel(*refs):
-    *refs, keep_ref, side_keep_ref, side_give_ref = refs
-    block_ref, side_ref, side_beside_ref, *others, gate_ref, up_ref, down_ref = refs
-    lows, highs = zip(*[halves(ref) for ref in (block_ref, *others)])
+def early_kernel(*refs):
+    *refs, keep_ref, give_ref, side_keep_ref, side_give_ref = refs
+    *others, side_ref, side_beside_ref, gate_ref, up_ref, down_ref = refs
+    lows, highs = zip(*[halves(ref) for ref in others])
     side_low, side_high = ordered(wide(side_ref), wide(side_beside_ref))
     hidden, coefficient = hidden_rows(
         [*lows, side_low], [*highs, side_high], gate_ref, up_ref
     )
     rows, width = keep_ref.shape
+    end = rows + give_ref.shape[0]
     half = width // 2
     step = half // 2
     for start in range(0, half, step):
         low = lowered(hidden, coefficient, down_ref, start, step)
         high = lowered(hidden, coefficient, down_ref, half + start, step)
-        keep_ref[:, start : start + step] = low[:rows]
-        keep_ref[:, half + start : half + start + step] = high[:rows]
-        keep, give = ordered(low[rows:], high[rows:])
+        for value, first in ((low, start), (high, half + start)):
+            keep_ref[:, first : first + step] = value[:rows]
+            give_ref[:, first : first + step] = value[rows:end].astype(jnp.bfloat16)
+        keep, give = ordered(low[end:], high[end:])
         side_keep_ref[:, start : start + step] = keep
         side_give_ref[:, start : start + step] = give.astype(jnp.bfloat16)
 
 
 def low_kernel(*refs):
-    *others, gate_ref, up_ref, down_ref, after_ref, give_ref, hidden_ref, coefficient_ref = refs
+    *others, gate_ref, up_ref, down_ref, give_ref, hidden_ref, coefficient_ref = refs
     lows, highs = zip(*[halves(ref) for ref in others])
     hidden, coefficient = hidden_rows(lows, highs, gate_ref, up_ref)
     hidden_ref[...] = hidden
     coefficient_ref[...] = jnp.broadcast_to(coefficient, coefficient_ref.shape)
-    half = give_ref.shape[1]
+    rows, half = give_ref.shape
     step = half // 2
     for start in range(0, half, step):
-        low = lowered(hidden, coefficient, down_ref, start, step)
+        low = lowered(hidden[:rows], coefficient[:rows], down_ref, start, step)
         give_ref[:, start : start + step] = low.astype(jnp.bfloat16)
 
 
 def high_kernel(hidden_ref, coefficient_ref, down_ref, give_ref):
-    hidden, coefficient = hidden_ref[...], coefficient_ref[:, :1]
-    half = give_ref.shape[1]
+    rows, half = give_ref.shape
+    hidden, coefficient = hidden_ref[:rows, :], coefficient_ref[:rows, :1]
     step = half // 2
     for start in range(0, half, step):
         high = lowered(hidden, coefficient, down_ref, half + start, step)
         give_ref[:, start : start + step] = high.astype(jnp.bfloat16)
 
 
-def fold_kernel(*refs):
-    keep_ref, low_ref, high_ref, side_keep_ref, side_other_ref, *outs, side_out_ref = refs
-    half = low_ref.shape[1]
+def kept_kernel(hidden_ref, coefficient_ref, down_ref, keep_ref):
+    rows, width = keep_ref.shape
+    hidden, coefficient = hidden_ref[rows:, :], coefficient_ref[rows:, :1]
+    step = width // 4
+    for start in range(0, width, step):
+        keep_ref[:, start : start + step] = lowered(hidden, coefficient, down_ref, start, step)
+
+
+def early_fold_kernel(*refs):
+    keep_ref, other_ref, side_keep_ref, side_other_ref, *outs, side_out_ref = refs
     count = side_out_ref.shape[0]
     side_out_ref[...] = (side_keep_ref[...] + wide(side_other_ref)).astype(jnp.bfloat16)
     for j, out_ref in enumerate(outs):
+        total = keep_ref[(j + 1) * count : (j + 2) * count, :]
+        total += other_ref[j * count : (j + 1) * count, :].astype(jnp.float32)
+        out_ref[...] = total.astype(jnp.bfloat16)
+
+
+def fold_kernel(*refs):
+    keep_ref, low_ref, high_ref, *outs = refs
+    half = low_ref.shape[1]
+    count = outs[0].shape[0]
+    for j, out_ref in enumerate(outs):
         rows = slice(j * count, (j + 1) * count)
-        kept = slice((j + 1) * count, (j + 2) * count)
-        low = keep_ref[kept, :half] + low_ref[rows, :].astype(jnp.float32)
-        high = keep_ref[kept, half:] + high_ref[rows, :].astype(jnp.float32)
+        low = keep_ref[rows, :half] + low_ref[rows, :].astype(jnp.float32)
+        high = keep_ref[rows, half:] + high_ref[rows, :].astype(jnp.float32)
         out_ref[:, :half] = low.astype(jnp.bfloat16)
         out_ref[:, half:] = high.astype(jnp.bfloat16)
 
@@ -291,15 +309,15 @@
     moved = swapped(packed, far)
     beside = swapped(packed, 1)
     weights = [pltpu.with_memory_space_constraint(w, pltpu.HBM) for w in (w_gate, w_up, w_down)]
-    gate, up, token = call(
+    *loaded, token = call(
         load_kernel,
-        [pltpu.VMEM(w.shape, w.dtype) for w in weights[:2]] + [shape((8, 128), f32)],
+        [pltpu.VMEM(w.shape, w.dtype) for w in weights] + [shape((8, 128), f32)],
         MIB,
-        *weights[:2],
-        specs=[HBM] * 2,
-        scratch=[pltpu.SemaphoreType.DMA((2,))],
-    )
-    gate, up = [pltpu.with_memory_space_constraint(w, pltpu.VMEM) for w in (gate, up)]
+        *weights,
+        specs=[HBM] * 3,
+        scratch=[pltpu.SemaphoreType.DMA((3,))],
+    )
+    loaded = [pltpu.with_memory_space_constraint(w, pltpu.VMEM) for w in loaded]
     rows = 4 * tokens
     block, side = call(
         combine_kernel,
@@ -316,72 +334,70 @@
     parts = [swapped(block, *step) for step in steps]
     side_beside = swapped(side, 1)
     beside = [swapped(part, 1) for part in parts]
-    count = len(steps)
+    early = early_count(devices)
+    late = len(steps) - early
     work = 2 * rows * width * inner
-    down, token = call(
-        load_kernel,
-        [pltpu.VMEM(w_down.shape, w_down.dtype), shape((8, 128), f32)],
-        MIB,
-        weights[2],
-        specs=[HBM],
-        scratch=[pltpu.SemaphoreType.DMA((1,))],
-    )
-    down = pltpu.with_memory_space_constraint(down, pltpu.VMEM)
-    keep, side_keep, side_give = call(
-        own_kernel,
+    keep, give, side_keep, side_give = call(
+        early_kernel,
         [
-            shape(((1 + count) * rows, width), f32),
+            shape(((1 + early) * rows, width), f32),
+            shape((early * rows, width), bf16),
             shape((rows, half), f32),
             shape((rows, half), bf16),
         ],
         16 * MIB,
         block,
+        *parts[:early],
+        *beside[:early],
         side,
         side_beside,
-        *parts,
-        gate,
-        up,
-        down,
-        flops=3 * (2 + count) * work,
-    )
-    side_give = swapped(side_give, 1)
+        *loaded,
+        flops=3 * (2 + 2 * early) * work,
+    )
+    *first_parts, side = call(
+        early_fold_kernel,
+        [shape((rows, width), bf16)] * early + [shape((rows, half), bf16)],
+        8 * MIB,
+        keep,
+        swapped(give, 1),
+        side_keep,
+        swapped(side_give, 1),
+    )
     low, hidden, coefficient = call(
         low_kernel,
         [
-            shape((count * rows, half), bf16),
-            shape((count * rows, inner), bf16),
-            shape((count * rows, 128), f32),
+            shape((late * rows, half), bf16),
+            shape((2 * late * rows, inner), bf16),
+            shape((2 * late * rows, 128), f32),
         ],
         16 * MIB,
-        *beside,
-        gate,
-        up,
-        down,
-        keep,
-        specs=[VMEM] * (3 + count) + [ANY],
-        flops=5 * count * work // 2,
+        *beside[early:],
+        *parts[early:],
+        *loaded,
+        flops=9 * late * work // 2,
     )
     low = swapped(low, 1)
     high = call(
         high_kernel,
-        [shape((count * rows, half), bf16)],
+        [shape((late * rows, half), bf16)],
         8 * MIB,
         hidden,
         coefficient,
-        down,
-        flops=count * work // 2,
+        loaded[2],
+        flops=late * work // 2,
     )
     high = swapped(high, 1)
-    *parts, side = call(
-        fold_kernel,
-        [shape((rows, width), bf16)] * count + [shape((rows, half), bf16)],
+    late_keep = call(
+        kept_kernel,
+        [shape((late * rows, width), f32)],
         8 * MIB,
-        keep,
-        low,
-        high,
-        side_keep,
-        side_give,
-    )
+        hidden,
+        coefficient,
+        loaded[2],
+        flops=late * work,
+    )
+    parts = call(fold_kernel, [shape((rows, width), bf16)] * late, 8 * MIB, late_keep, low, high)
+    parts = [*first_parts, *parts]
     side = swapped(side, shared)
     parts = [swapped(part, *step) for part, step in zip(parts, steps)]
     mine, give = call(
@@ -400,6 +416,10 @@
         swapped(give, 1),
     )
     return call(finish_kernel, [shape((tokens, width), bf16)], 4 * MIB, near, swapped(give, far))
+
+
+def early_count(devices):
+    return max(1, (devices // 8 - 1) // 3)
 
 
 def solution(mesh):

time: 53.6 us -> 52.8 us (0.985)
  waiting for transfers between devices: 17.3 us -> 19.1 us
  starting transfers between devices: 23.9 us -> 22.3 us
  Pallas kernels: 12 us -> 11.1 us
    ppermute x20 -> x21, waiting for transfers between devices: 17.3 us -> 19.1 us  [swapped(): return lax.ppermute(array, 'ep', pairs)]
    ppermute x20 -> x21, starting transfers between devices: 23.9 us -> 22.3 us  [swapped(): return lax.ppermute(array, 'ep', pairs)]
    pallas_call x11 -> x12, Pallas kernels: 12 us -> 11.1 us  [call(): pl.pallas_call(kernel, out_shape=outs[0] if single else tuple(outs), in_s...]
  transfers between devices with their start and end apart: 20 -> 21, of which waited for: 6 -> 8; matrix products, arithmetic and copies ran while one was open for 0% -> 0% of each run, Pallas kernels for 14% -> 17%
where the time goes in v1:
time: 52.8 us; the launch traced here: 52.7 us
  starting transfers between devices  22.3 us (42%)
  waiting for transfers between devices  19.1 us (36%)
  Pallas kernels  11.1 us (21%)
    ppermute x21, starting transfers between devices, swapped(): return lax.ppermute(array, 'ep', pairs)  22.3 us
    ppermute x21, waiting for transfers between devices, swapped(): return lax.ppermute(array, 'ep', pairs)  19.1 us
    pallas_call x12, Pallas kernels, call(): pl.pallas_call(kernel, out_shape=outs[0] if single else tuple(outs), in_s...  11.1 us
  transfers between devices with their start and end apart: 21, of which 8 were waited for; matrix products, arithmetic and copies ran while one was open for 0% of the time, Pallas kernels for 17%

profile of v1, /device:TPU:0, one launch (start us, length us, event | category | flops | bytes accessed | tf_op | source)
XLA Modules:
  0.0 52.7 jit_solution(5982741647791544370)
XLA Ops:
  0.0 1.1 %shard_map.82.own_ref = bf16[24,1024]{1,0:T(8,128)(2,1)S(1)} custom-call(s32[2]{0:T(128)} %draft_hbm.1, bf16[6,3584]{1,0:T(8,128)(2,1)} %states_hbm.1, f32[3584]{0:T(1024)} %gain_hbm.1, f32[6,8]{1,0:T(8,128)} %scores_hbm.1, s32[6,8]{1,0:T(8,128)} %routes_hbm.1), custom_call_target="tpu_custom_call" | custom-call | bytes 106888 | tf_op jit(solution)/shard_map/pallas_call | solution.py:44
  1.1 4.1 %collective-permute-start.1 = (bf16[24,1024]{1,0:T(8,128)(2,1)S(1)}, bf16[24,1024]{1,0:T(8,128)(2,1)S(1)}, u32[]{:S(2)}, u32[]{:S(2)}) collective-permute-start(bf16[24,1024]{1,0:T(8,128)(2,1)S(1)} %shard_map.82.own_ref), channel_id=1, source_target_pairs={{0,16},{1,17},{2,18},{3,19},{4,20},{5,21},{6,22},{7,23},{8,24},{9,... | collective-permute-start | bytes 147464 | tf_op jit(solution)/shard_map/ppermute | solution.py:21
  5.2 2.6 %collective-permute-done.1.far_ref = bf16[24,1024]{1,0:T(8,128)(2,1)S(1)} collective-permute-done((bf16[24,1024]{1,0:T(8,128)(2,1)S(1)}, bf16[24,1024]{1,0:T(8,128)(2,1)S(1)}, u32[]{:S(2)}, u32[]{:S(2)}) %collective-permute-start.1) | collective-permute-done | bytes 49184 | tf_op jit(solution)/shard_map/ppermute | solution.py:21
  7.8 4.2 %shard_map.83 = (bf16[1,3584,512]{2,1,0:T(8,128)(2,1)S(1)}, bf16[1,3584,512]{2,1,0:T(8,128)(2,1)S(1)}, bf16[1,512,3584]{2,1,0:T(8,128)(2,1)S(1)}, f32[8,128]{1,0:T(8,128)S(1)}) custom-call(bf16[1,3584,512]{2,1,0:T(8,128)(2,1)} %refs_0_.1, bf16[1,3584,512]{2,1,0:T(8,128)(2,1)} %refs_1_.1, bf16[1,512,3584]{2,1,0:T(8,128)(2,1)} %refs_2_.1), custom_call_target="tpu_custom_call" | custom-call | bytes 22024192 | tf_op jit(solution)/shard_map/pallas_call | solution.py:44
  12.2 1.8 %collective-permute-start.3 = (bf16[24,3840]{1,0:T(8,128)(2,1)S(1)}, bf16[24,3840]{1,0:T(8,128)(2,1)S(1)}, u32[]{:S(2)}, u32[]{:S(2)}) collective-permute-start(bf16[24,3840]{1,0:T(8,128)(2,1)S(1)} %get-tuple-element.27.refs_0_), channel_id=1, source_target_pairs={{0,2},{1,13},{2,0},{3,15},{4,6},{5,9},{6,4},{7,11},{8,10},{9,5},{1... | collective-permute-start | bytes 552968 | tf_op jit(solution)/shard_map/ppermute | solution.py:21
  13.9 1.5 %collective-permute-start.11 = (bf16[24,3840]{1,0:T(8,128)(2,1)S(1)}, bf16[24,3840]{1,0:T(8,128)(2,1)S(1)}, u32[]{:S(2)}, u32[]{:S(2)}) collective-permute-start(bf16[24,3840]{1,0:T(8,128)(2,1)S(1)} %get-tuple-element.27.refs_0_), channel_id=1, source_target_pairs={{0,4},{1,11},{2,6},{3,9},{4,0},{5,15},{6,2},{7,13},{8,12},{9,3},{1... | collective-permute-start | bytes 552968 | tf_op jit(solution)/shard_map/ppermute | solution.py:21
  15.7 3.3 %collective-permute-start.5 = (bf16[24,1920]{1,0:T(8,128)(2,1)S(1)}, bf16[24,1920]{1,0:T(8,128)(2,1)S(1)}, u32[]{:S(2)}, u32[]{:S(2)}) collective-permute-start(bf16[24,1920]{1,0:T(8,128)(2,1)S(1)} %get-tuple-element.28), channel_id=1, source_target_pairs={{0,14},{1,15},{2,12},{3,13},{4,10},{5,11},{6,8},{7,9},{8,6},{9,7},... | collective-permute-start | bytes 276488 | tf_op jit(solution)/shard_map/ppermute | solution.py:21
  19.0 4.1 %collective-permute-done.5.refs_3_ = bf16[24,1920]{1,0:T(8,128)(2,1)S(1)} collective-permute-done((bf16[24,1920]{1,0:T(8,128)(2,1)S(1)}, bf16[24,1920]{1,0:T(8,128)(2,1)S(1)}, u32[]{:S(2)}, u32[]{:S(2)}) %collective-permute-start.5) | collective-permute-done | bytes 92192 | tf_op jit(solution)/shard_map/ppermute | solution.py:21
  23.1 2.1 %collective-permute-start.6 = (bf16[24,1920]{1,0:T(8,128)(2,1)S(1)}, bf16[24,1920]{1,0:T(8,128)(2,1)S(1)}, u32[]{:S(2)}, u32[]{:S(2)}) collective-permute-start(bf16[24,1920]{1,0:T(8,128)(2,1)S(1)} %collective-permute-done.5.refs_3_), channel_id=1, source_target_pairs={{0,1},{1,0},{2,3},{3,2},{4,5},{5,4},{6,7},{7,6},{8,9},{9,8},{10,11... | collective-permute-start | bytes 276488 | tf_op jit(solution)/shard_map/ppermute | solution.py:21
  25.2 0.5 collective-permute-start.14
  25.7 0.4 collective-permute-done.6.refs_4_
  26.1 1.9 %shard_map.85 = (f32[48,3584]{1,0:T(8,128)S(1)}, bf16[24,3584]{1,0:T(8,128)(2,1)S(1)}, f32[24,1792]{1,0:T(8,128)S(1)}, bf16[24,1792]{1,0:T(8,128)(2,1)S(1)}) custom-call(bf16[24,3840]{1,0:T(8,128)(2,1)S(1)} %get-tuple-element.27.refs_0_, bf16[24,3840]{1,0:T(8,128)(2,1)S(1)} %collective-permute-done.3.refs_1_, ...), custom_call_target="tpu_custom_call" | custom-call | flops 1056964608 | bytes 12865536 | tf_op jit(solution)/shard_map/pallas_call | solution.py:44
  28.5 1.7 %shard_map.87 = (bf16[48,1792]{1,0:T(8,128)(2,1)S(1)}, bf16[96,512]{1,0:T(8,128)(2,1)S(1)}, f32[96,128]{1,0:T(8,128)S(1)}) custom-call(bf16[24,3840]{1,0:T(8,128)(2,1)S(1)} %collective-permute-done.12.refs_0_, bf16[24,3840]{1,0:T(8,128)(2,1)S(1)} %collective-permute-done.14.refs_1_, bf16[24,3840]{1,0:T(8,128)(2,1)S(1)} %collective-permute-done.11.refs_2_, ...), custom_call_target="tpu_custom_call" | custom-call | flops 792723456 | bytes 12066816 | tf_op jit(solution)/shard_map/pallas_call | solution.py:44
  31.4 0.7 %shard_map.88.refs_0_ = f32[48,3584]{1,0:T(8,128)S(1)} custom-call(bf16[96,512]{1,0:T(8,128)(2,1)S(1)} %get-tuple-element.38.hidden_ref, f32[96,128]{1,0:T(8,128)S(1)} %get-tuple-element.39.coefficient_ref, bf16[1,512,3584]{2,1,0:T(8,128)(2,1)S(1)} %get-tuple-element.31.refs_7_.refs_6_.down_ref), custom_call_target="tpu_custom_call" | custom-call | flops 176160768 | bytes 4505600 | tf_op jit(solution)/shard_map/pallas_call | solution.py:44
  32.5 0.5 collective-permute-start.10
  33.2 1.6 %collective-permute-start.17 = (bf16[24,3584]{1,0:T(8,128)(2,1)S(1)}, bf16[24,3584]{1,0:T(8,128)(2,1)S(1)}, u32[]{:S(2)}, u32[]{:S(2)}) collective-permute-start(bf16[24,3584]{1,0:T(8,128)(2,1)S(1)} %get-tuple-element.41), channel_id=1, source_target_pairs={{0,4},{1,11},{2,6},{3,9},{4,0},{5,15},{6,2},{7,13},{8,12},{9,3},{1... | collective-permute-start | bytes 516104 | tf_op jit(solution)/shard_map/ppermute | solution.py:21
  34.8 1.5 %collective-permute-start.18 = (bf16[24,3584]{1,0:T(8,128)(2,1)S(1)}, bf16[24,3584]{1,0:T(8,128)(2,1)S(1)}, u32[]{:S(2)}, u32[]{:S(2)}) collective-permute-start(bf16[24,3584]{1,0:T(8,128)(2,1)S(1)} %get-tuple-element.42), channel_id=1, source_target_pairs={{0,6},{1,9},{2,4},{3,11},{4,2},{5,13},{6,0},{7,15},{8,14},{9,1},{1... | collective-permute-start | bytes 516104 | tf_op jit(solution)/shard_map/ppermute | solution.py:21
  36.3 2.1 %collective-permute-start.9 = (bf16[24,1792]{1,0:T(8,128)(2,1)S(1)}, bf16[24,1792]{1,0:T(8,128)(2,1)S(1)}, u32[]{:S(2)}, u32[]{:S(2)}) collective-permute-start(bf16[24,1792]{1,0:T(8,128)(2,1)S(1)} %get-tuple-element.36), channel_id=1, source_target_pairs={{0,14},{1,15},{2,12},{3,13},{4,10},{5,11},{6,8},{7,9},{8,6},{9,7},... | collective-permute-start | bytes 258056 | tf_op jit(solution)/shard_map/ppermute | solution.py:21
  38.3 5.2 %collective-permute-done.9.refs_1_ = bf16[24,1792]{1,0:T(8,128)(2,1)S(1)} collective-permute-done((bf16[24,1792]{1,0:T(8,128)(2,1)S(1)}, bf16[24,1792]{1,0:T(8,128)(2,1)S(1)}, u32[]{:S(2)}, u32[]{:S(2)}) %collective-permute-start.9) | collective-permute-done | bytes 86048 | tf_op jit(solution)/shard_map/ppermute | solution.py:21
  43.6 1.0 %collective-permute-done.18.refs_4_ = bf16[24,3584]{1,0:T(8,128)(2,1)S(1)} collective-permute-done((bf16[24,3584]{1,0:T(8,128)(2,1)S(1)}, bf16[24,3584]{1,0:T(8,128)(2,1)S(1)}, u32[]{:S(2)}, u32[]{:S(2)}) %collective-permute-start.18) | collective-permute-done | bytes 172064 | tf_op jit(solution)/shard_map/ppermute | solution.py:21
  44.8 1.3 %collective-permute-done.19.other_ref = bf16[24,1792]{1,0:T(8,128)(2,1)S(1)} collective-permute-done((bf16[24,1792]{1,0:T(8,128)(2,1)S(1)}, bf16[24,1792]{1,0:T(8,128)(2,1)S(1)}, u32[]{:S(2)}, u32[]{:S(2)}) %collective-permute-start.19) | collective-permute-done | bytes 86048 | tf_op jit(solution)/shard_map/ppermute | solution.py:21
  46.1 1.8 %collective-permute-start.20 = (bf16[24,896]{1,0:T(8,128)(2,1)S(1)}, bf16[24,896]{1,0:T(8,128)(2,1)S(1)}, u32[]{:S(2)}, u32[]{:S(2)}) collective-permute-start(bf16[24,896]{1,0:T(8,128)(2,1)S(1)} %get-tuple-element.46), channel_id=1, source_target_pairs={{0,16},{1,17},{2,18},{3,19},{4,20},{5,21},{6,22},{7,23},{8,24},{9,... | collective-permute-start | bytes 129032 | tf_op jit(solution)/shard_map/ppermute | solution.py:21
  47.9 4.1 %collective-permute-done.20.other_ref = bf16[24,896]{1,0:T(8,128)(2,1)S(1)} collective-permute-done((bf16[24,896]{1,0:T(8,128)(2,1)S(1)}, bf16[24,896]{1,0:T(8,128)(2,1)S(1)}, u32[]{:S(2)}, u32[]{:S(2)}) %collective-permute-start.20) | collective-permute-done | bytes 43040 | tf_op jit(solution)/shard_map/ppermute | solution.py:21
  52.0 0.6 %shard_map.93 = bf16[6,3584]{1,0:T(8,128)(2,1)} custom-call(f32[24,896]{1,0:T(8,128)S(1)} %get-tuple-element.45.near_ref, bf16[24,896]{1,0:T(8,128)(2,1)S(1)} %collective-permute-done.20.other_ref), custom_call_target="tpu_custom_call" | custom-call | bytes 172032 | tf_op jit(solution)/shard_map/pallas_call | solution.py:44
  (30 shorter events, 2.9 us)
Async XLA Ops:
  1.1 6.7 %collective-permute-start.1 = (bf16[24,1024]{1,0:T(8,128)(2,1)S(1)}, bf16[24,1024]{1,0:T(8,128)(2,1)S(1)}, u32[]{:S(2)}, u32[]{:S(2)}) collective-permute-start(bf16[24,1024]{1,0:T(8,128)(2,1)S(1)} %shard_map.82.own_ref), channel_id=1, source_target_pairs={{0,16},{1,17},{2,18},{3,19},{4,20},{5,21},{6,22},{7,23},{8,24},{9,... | collective-permute-start | bytes 147464 | tf_op jit(solution)/shard_map/ppermute | solution.py:21
  5.2 6.8 %collective-permute-start = (bf16[24,1024]{1,0:T(8,128)(2,1)S(1)}, bf16[24,1024]{1,0:T(8,128)(2,1)S(1)}, u32[]{:S(2)}, u32[]{:S(2)}) collective-permute-start(bf16[24,1024]{1,0:T(8,128)(2,1)S(1)} %shard_map.82.own_ref), channel_id=1, source_target_pairs={{0,1},{1,0},{2,3},{3,2},{4,5},{5,4},{6,7},{7,6},{8,9},{9,8},{10,11... | collective-permute-start | bytes 147464 | tf_op jit(solution)/shard_map/ppermute | solution.py:21
  7.8 4.3 %collective-permute-start.2 = (bf16[24,1024]{1,0:T(8,128)(2,1)S(1)}, bf16[24,1024]{1,0:T(8,128)(2,1)S(1)}, u32[]{:S(2)}, u32[]{:S(2)}) collective-permute-start(bf16[24,1024]{1,0:T(8,128)(2,1)S(1)} %collective-permute-done.1.far_ref), channel_id=1, source_target_pairs={{0,1},{1,0},{2,3},{3,2},{4,5},{5,4},{6,7},{7,6},{8,9},{9,8},{10,11... | collective-permute-start | bytes 147464 | tf_op jit(solution)/shard_map/ppermute | solution.py:21
  12.2 6.8 %collective-permute-start.3 = (bf16[24,3840]{1,0:T(8,128)(2,1)S(1)}, bf16[24,3840]{1,0:T(8,128)(2,1)S(1)}, u32[]{:S(2)}, u32[]{:S(2)}) collective-permute-start(bf16[24,3840]{1,0:T(8,128)(2,1)S(1)} %get-tuple-element.27.refs_0_), channel_id=1, source_target_pairs={{0,2},{1,13},{2,0},{3,15},{4,6},{5,9},{6,4},{7,11},{8,10},{9,5},{1... | collective-permute-start | bytes 552968 | tf_op jit(solution)/shard_map/ppermute | solution.py:21
  13.9 11.2 %collective-permute-start.11 = (bf16[24,3840]{1,0:T(8,128)(2,1)S(1)}, bf16[24,3840]{1,0:T(8,128)(2,1)S(1)}, u32[]{:S(2)}, u32[]{:S(2)}) collective-permute-start(bf16[24,3840]{1,0:T(8,128)(2,1)S(1)} %get-tuple-element.27.refs_0_), channel_id=1, source_target_pairs={{0,4},{1,11},{2,6},{3,9},{4,0},{5,15},{6,2},{7,13},{8,12},{9,3},{1... | collective-permute-start | bytes 552968 | tf_op jit(solution)/shard_map/ppermute | solution.py:21
  15.5 9.7 %collective-permute-start.13 = (bf16[24,3840]{1,0:T(8,128)(2,1)S(1)}, bf16[24,3840]{1,0:T(8,128)(2,1)S(1)}, u32[]{:S(2)}, u32[]{:S(2)}) collective-permute-start(bf16[24,3840]{1,0:T(8,128)(2,1)S(1)} %get-tuple-element.27.refs_0_), channel_id=1, source_target_pairs={{0,6},{1,9},{2,4},{3,11},{4,2},{5,13},{6,0},{7,15},{8,14},{9,1},{1... | collective-permute-start | bytes 552968 | tf_op jit(solution)/shard_map/ppermute | solution.py:21
  15.7 7.4 %collective-permute-start.5 = (bf16[24,1920]{1,0:T(8,128)(2,1)S(1)}, bf16[24,1920]{1,0:T(8,128)(2,1)S(1)}, u32[]{:S(2)}, u32[]{:S(2)}) collective-permute-start(bf16[24,1920]{1,0:T(8,128)(2,1)S(1)} %get-tuple-element.28), channel_id=1, source_target_pairs={{0,14},{1,15},{2,12},{3,13},{4,10},{5,11},{6,8},{7,9},{8,6},{9,7},... | collective-permute-start | bytes 276488 | tf_op jit(solution)/shard_map/ppermute | solution.py:21
  19.0 7.1 %collective-permute-start.4 = (bf16[24,3840]{1,0:T(8,128)(2,1)S(1)}, bf16[24,3840]{1,0:T(8,128)(2,1)S(1)}, u32[]{:S(2)}, u32[]{:S(2)}) collective-permute-start(bf16[24,3840]{1,0:T(8,128)(2,1)S(1)} %collective-permute-done.3.refs_1_), channel_id=1, source_target_pairs={{0,1},{1,0},{2,3},{3,2},{4,5},{5,4},{6,7},{7,6},{8,9},{9,8},{10,11... | collective-permute-start | bytes 552968 | tf_op jit(solution)/shard_map/ppermute | solution.py:21
  23.1 3.0 %collective-permute-start.6 = (bf16[24,1920]{1,0:T(8,128)(2,1)S(1)}, bf16[24,1920]{1,0:T(8,128)(2,1)S(1)}, u32[]{:S(2)}, u32[]{:S(2)}) collective-permute-start(bf16[24,1920]{1,0:T(8,128)(2,1)S(1)} %collective-permute-done.5.refs_3_), channel_id=1, source_target_pairs={{0,1},{1,0},{2,3},{3,2},{4,5},{5,4},{6,7},{7,6},{8,9},{9,8},{10,11... | collective-permute-start | bytes 276488 | tf_op jit(solution)/shard_map/ppermute | solution.py:21
  25.2 3.3 %collective-permute-start.12 = (bf16[24,3840]{1,0:T(8,128)(2,1)S(1)}, bf16[24,3840]{1,0:T(8,128)(2,1)S(1)}, u32[]{:S(2)}, u32[]{:S(2)}) collective-permute-start(bf16[24,3840]{1,0:T(8,128)(2,1)S(1)} %collective-permute-done.11.refs_2_), channel_id=1, source_target_pairs={{0,1},{1,0},{2,3},{3,2},{4,5},{5,4},{6,7},{7,6},{8,9},{9,8},{10,11... | collective-permute-start | bytes 552968 | tf_op jit(solution)/shard_map/ppermute | solution.py:21
  25.2 3.3 %collective-permute-start.14 = (bf16[24,3840]{1,0:T(8,128)(2,1)S(1)}, bf16[24,3840]{1,0:T(8,128)(2,1)S(1)}, u32[]{:S(2)}, u32[]{:S(2)}) collective-permute-start(bf16[24,3840]{1,0:T(8,128)(2,1)S(1)} %collective-permute-done.13.refs_3_), channel_id=1, source_target_pairs={{0,1},{1,0},{2,3},{3,2},{4,5},{5,4},{6,7},{7,6},{8,9},{9,8},{10,11... | collective-permute-start | bytes 552968 | tf_op jit(solution)/shard_map/ppermute | solution.py:21
  28.1 4.4 %collective-permute-start.7 = (bf16[24,3584]{1,0:T(8,128)(2,1)S(1)}, bf16[24,3584]{1,0:T(8,128)(2,1)S(1)}, u32[]{:S(2)}, u32[]{:S(2)}) collective-permute-start(bf16[24,3584]{1,0:T(8,128)(2,1)S(1)} %get-tuple-element.33), channel_id=1, source_target_pairs={{0,1},{1,0},{2,3},{3,2},{4,5},{5,4},{6,7},{7,6},{8,9},{9,8},{10,11... | collective-permute-start | bytes 516104 | tf_op jit(solution)/shard_map/ppermute | solution.py:21
  30.1 2.9 %collective-permute-start.15 = (bf16[48,1792]{1,0:T(8,128)(2,1)S(1)}, bf16[48,1792]{1,0:T(8,128)(2,1)S(1)}, u32[]{:S(2)}, u32[]{:S(2)}) collective-permute-start(bf16[48,1792]{1,0:T(8,128)(2,1)S(1)} %get-tuple-element.40), channel_id=1, source_target_pairs={{0,1},{1,0},{2,3},{3,2},{4,5},{5,4},{6,7},{7,6},{8,9},{9,8},{10,11... | collective-permute-start | bytes 516104 | tf_op jit(solution)/shard_map/ppermute | solution.py:21
  30.8 2.3 %collective-permute-start.16 = (bf16[48,1792]{1,0:T(8,128)(2,1)S(1)}, bf16[48,1792]{1,0:T(8,128)(2,1)S(1)}, u32[]{:S(2)}, u32[]{:S(2)}) collective-permute-start(bf16[48,1792]{1,0:T(8,128)(2,1)S(1)} %shard_map.89), channel_id=1, source_target_pairs={{0,1},{1,0},{2,3},{3,2},{4,5},{5,4},{6,7},{7,6},{8,9},{9,8},{10,11... | collective-permute-start | bytes 516104 | tf_op jit(solution)/shard_map/ppermute | solution.py:21
  31.2 1.3 %collective-permute-start.8 = (bf16[24,1792]{1,0:T(8,128)(2,1)S(1)}, bf16[24,1792]{1,0:T(8,128)(2,1)S(1)}, u32[]{:S(2)}, u32[]{:S(2)}) collective-permute-start(bf16[24,1792]{1,0:T(8,128)(2,1)S(1)} %get-tuple-element.35), channel_id=1, source_target_pairs={{0,1},{1,0},{2,3},{3,2},{4,5},{5,4},{6,7},{7,6},{8,9},{9,8},{10,11... | collective-permute-start | bytes 258056 | tf_op jit(solution)/shard_map/ppermute | solution.py:21
  32.5 11.0 %collective-permute-start.10 = (bf16[24,3584]{1,0:T(8,128)(2,1)S(1)}, bf16[24,3584]{1,0:T(8,128)(2,1)S(1)}, u32[]{:S(2)}, u32[]{:S(2)}) collective-permute-start(bf16[24,3584]{1,0:T(8,128)(2,1)S(1)} %get-tuple-element.37), channel_id=1, source_target_pairs={{0,2},{1,13},{2,0},{3,15},{4,6},{5,9},{6,4},{7,11},{8,10},{9,5},{1... | collective-permute-start | bytes 516104 | tf_op jit(solution)/shard_map/ppermute | solution.py:21
  33.2 10.4 %collective-permute-start.17 = (bf16[24,3584]{1,0:T(8,128)(2,1)S(1)}, bf16[24,3584]{1,0:T(8,128)(2,1)S(1)}, u32[]{:S(2)}, u32[]{:S(2)}) collective-permute-start(bf16[24,3584]{1,0:T(8,128)(2,1)S(1)} %get-tuple-element.41), channel_id=1, source_target_pairs={{0,4},{1,11},{2,6},{3,9},{4,0},{5,15},{6,2},{7,13},{8,12},{9,3},{1... | collective-permute-start | bytes 516104 | tf_op jit(solution)/shard_map/ppermute | solution.py:21
  34.8 9.7 %collective-permute-start.18 = (bf16[24,3584]{1,0:T(8,128)(2,1)S(1)}, bf16[24,3584]{1,0:T(8,128)(2,1)S(1)}, u32[]{:S(2)}, u32[]{:S(2)}) collective-permute-start(bf16[24,3584]{1,0:T(8,128)(2,1)S(1)} %get-tuple-element.42), channel_id=1, source_target_pairs={{0,6},{1,9},{2,4},{3,11},{4,2},{5,13},{6,0},{7,15},{8,14},{9,1},{1... | collective-permute-start | bytes 516104 | tf_op jit(solution)/shard_map/ppermute | solution.py:21
  36.3 7.3 %collective-permute-start.9 = (bf16[24,1792]{1,0:T(8,128)(2,1)S(1)}, bf16[24,1792]{1,0:T(8,128)(2,1)S(1)}, u32[]{:S(2)}, u32[]{:S(2)}) collective-permute-start(bf16[24,1792]{1,0:T(8,128)(2,1)S(1)} %get-tuple-element.36), channel_id=1, source_target_pairs={{0,14},{1,15},{2,12},{3,13},{4,10},{5,11},{6,8},{7,9},{8,6},{9,7},... | collective-permute-start | bytes 258056 | tf_op jit(solution)/shard_map/ppermute | solution.py:21
  44.7 1.3 %collective-permute-start.19 = (bf16[24,1792]{1,0:T(8,128)(2,1)S(1)}, bf16[24,1792]{1,0:T(8,128)(2,1)S(1)}, u32[]{:S(2)}, u32[]{:S(2)}) collective-permute-start(bf16[24,1792]{1,0:T(8,128)(2,1)S(1)} %get-tuple-element.44), channel_id=1, source_target_pairs={{0,1},{1,0},{2,3},{3,2},{4,5},{5,4},{6,7},{7,6},{8,9},{9,8},{10,11... | collective-permute-start | bytes 258056 | tf_op jit(solution)/shard_map/ppermute | solution.py:21
  46.1 5.9 %collective-permute-start.20 = (bf16[24,896]{1,0:T(8,128)(2,1)S(1)}, bf16[24,896]{1,0:T(8,128)(2,1)S(1)}, u32[]{:S(2)}, u32[]{:S(2)}) collective-permute-start(bf16[24,896]{1,0:T(8,128)(2,1)S(1)} %get-tuple-element.46), channel_id=1, source_target_pairs={{0,16},{1,17},{2,18},{3,19},{4,20},{5,21},{6,22},{7,23},{8,24},{9,... | collective-permute-start | bytes 129032 | tf_op jit(solution)/shard_map/ppermute | solution.py:21

commit v2 on v1

--- a/solution.py
+++ b/solution.py
@@ -181,34 +181,16 @@
         side_give_ref[:, start : start + step] = give.astype(jnp.bfloat16)
 
 
-def low_kernel(*refs):
-    *others, gate_ref, up_ref, down_ref, give_ref, hidden_ref, coefficient_ref = refs
+def late_kernel(*refs):
+    *others, gate_ref, up_ref, down_ref, keep_ref, give_ref = refs
     lows, highs = zip(*[halves(ref) for ref in others])
     hidden, coefficient = hidden_rows(lows, highs, gate_ref, up_ref)
-    hidden_ref[...] = hidden
-    coefficient_ref[...] = jnp.broadcast_to(coefficient, coefficient_ref.shape)
-    rows, half = give_ref.shape
-    step = half // 2
-    for start in range(0, half, step):
-        low = lowered(hidden[:rows], coefficient[:rows], down_ref, start, step)
-        give_ref[:, start : start + step] = low.astype(jnp.bfloat16)
-
-
-def high_kernel(hidden_ref, coefficient_ref, down_ref, give_ref):
-    rows, half = give_ref.shape
-    hidden, coefficient = hidden_ref[:rows, :], coefficient_ref[:rows, :1]
-    step = half // 2
-    for start in range(0, half, step):
-        high = lowered(hidden, coefficient, down_ref, half + start, step)
-        give_ref[:, start : start + step] = high.astype(jnp.bfloat16)
-
-
-def kept_kernel(hidden_ref, coefficient_ref, down_ref, keep_ref):
     rows, width = keep_ref.shape
-    hidden, coefficient = hidden_ref[rows:, :], coefficient_ref[rows:, :1]
     step = width // 4
     for start in range(0, width, step):
-        keep_ref[:, start : start + step] = lowered(hidden, coefficient, down_ref, start, step)
+        partial = lowered(hidden, coefficient, down_ref, start, step)
+        keep_ref[:, start : start + step] = partial[:rows]
+        give_ref[:, start : start + step] = partial[rows:].astype(jnp.bfloat16)
 
 
 def early_fold_kernel(*refs):
@@ -221,16 +203,12 @@
         out_ref[...] = total.astype(jnp.bfloat16)
 
 
-def fold_kernel(*refs):
-    keep_ref, low_ref, high_ref, *outs = refs
-    half = low_ref.shape[1]
+def fold_kernel(keep_ref, other_ref, *outs):
     count = outs[0].shape[0]
     for j, out_ref in enumerate(outs):
         rows = slice(j * count, (j + 1) * count)
-        low = keep_ref[rows, :half] + low_ref[rows, :].astype(jnp.float32)
-        high = keep_ref[rows, half:] + high_ref[rows, :].astype(jnp.float32)
-        out_ref[:, :half] = low.astype(jnp.bfloat16)
-        out_ref[:, half:] = high.astype(jnp.bfloat16)
+        total = keep_ref[rows, :] + other_ref[rows, :].astype(jnp.float32)
+        out_ref[...] = total.astype(jnp.bfloat16)
 
 
 def sum_kernel(*refs):
@@ -363,40 +341,18 @@
         side_keep,
         swapped(side_give, 1),
     )
-    low, hidden, coefficient = call(
-        low_kernel,
-        [
-            shape((late * rows, half), bf16),
-            shape((2 * late * rows, inner), bf16),
-            shape((2 * late * rows, 128), f32),
-        ],
+    late_keep, late_give = call(
+        late_kernel,
+        [shape((late * rows, width), f32), shape((late * rows, width), bf16)],
         16 * MIB,
+        *parts[early:],
         *beside[early:],
-        *parts[early:],
         *loaded,
-        flops=9 * late * work // 2,
-    )
-    low = swapped(low, 1)
-    high = call(
-        high_kernel,
-        [shape((late * rows, half), bf16)],
-        8 * MIB,
-        hidden,
-        coefficient,
-        loaded[2],
-        flops=late * work // 2,
-    )
-    high = swapped(high, 1)
-    late_keep = call(
-        kept_kernel,
-        [shape((late * rows, width), f32)],
-        8 * MIB,
-        hidden,
-        coefficient,
-        loaded[2],
-        flops=late * work,
-    )
-    parts = call(fold_kernel, [shape((rows, width), bf16)] * late, 8 * MIB, late_keep, low, high)
+        flops=6 * late * work,
+    )
+    parts = call(
+        fold_kernel, [shape((rows, width), bf16)] * late, 8 * MIB, late_keep, swapped(late_give, 1)
+    )
     parts = [*first_parts, *parts]
     side = swapped(side, shared)
     parts = [swapped(part, *step) for part, step in zip(parts, steps)]

time: 52.8 us -> 54.4 us (1.030)
  waiting for transfers between devices: 19.1 us -> 22 us
  Pallas kernels: 11.1 us -> 10.3 us
    ppermute x21 -> x20, waiting for transfers between devices: 19.1 us -> 22 us  [swapped(): return lax.ppermute(array, 'ep', pairs)]
    pallas_call x12 -> x10, Pallas kernels: 11.1 us -> 10.3 us  [call(): pl.pallas_call(kernel, out_shape=outs[0] if single else tuple(outs), in_s...]
    ppermute x21 -> x20, starting transfers between devices: 22.3 us -> 21.9 us  [swapped(): return lax.ppermute(array, 'ep', pairs)]
  transfers between devices with their start and end apart: 21 -> 20, of which waited for: 8 -> 9; matrix products, arithmetic and copies ran while one was open for 0% -> 0% of each run, Pallas kernels for 17% -> 15%
where the time goes in v2:
time: 54.4 us; the launch traced here: 54.2 us
  waiting for transfers between devices  22 us (40%)
  starting transfers between devices  21.9 us (40%)
  Pallas kernels  10.3 us (19%)
    ppermute x20, waiting for transfers between devices, swapped(): return lax.ppermute(array, 'ep', pairs)  22 us
    ppermute x20, starting transfers between devices, swapped(): return lax.ppermute(array, 'ep', pairs)  21.9 us
    pallas_call x10, Pallas kernels, call(): pl.pallas_call(kernel, out_shape=outs[0] if single else tuple(outs), in_s...  10.3 us
  transfers between devices with their start and end apart: 20, of which 9 were waited for; matrix products, arithmetic and copies ran while one was open for 0% of the time, Pallas kernels for 15%

profile of v2, /device:TPU:0, one launch (start us, length us, event | category | flops | bytes accessed | tf_op | source)
XLA Modules:
  0.0 54.2 jit_solution(14757105585177223817)
XLA Ops:
  0.0 1.1 %shard_map.82.own_ref = bf16[24,1024]{1,0:T(8,128)(2,1)S(1)} custom-call(s32[2]{0:T(128)} %draft_hbm.1, bf16[6,3584]{1,0:T(8,128)(2,1)} %states_hbm.1, f32[3584]{0:T(1024)} %gain_hbm.1, f32[6,8]{1,0:T(8,128)} %scores_hbm.1, s32[6,8]{1,0:T(8,128)} %routes_hbm.1), custom_call_target="tpu_custom_call" | custom-call | bytes 106888 | tf_op jit(solution)/shard_map/pallas_call | solution.py:44
  1.1 4.1 %collective-permute-start.1 = (bf16[24,1024]{1,0:T(8,128)(2,1)S(1)}, bf16[24,1024]{1,0:T(8,128)(2,1)S(1)}, u32[]{:S(2)}, u32[]{:S(2)}) collective-permute-start(bf16[24,1024]{1,0:T(8,128)(2,1)S(1)} %shard_map.82.own_ref), channel_id=1, source_target_pairs={{0,16},{1,17},{2,18},{3,19},{4,20},{5,21},{6,22},{7,23},{8,24},{9,... | collective-permute-start | bytes 147464 | tf_op jit(solution)/shard_map/ppermute | solution.py:21
  5.2 2.6 %collective-permute-done.1.far_ref = bf16[24,1024]{1,0:T(8,128)(2,1)S(1)} collective-permute-done((bf16[24,1024]{1,0:T(8,128)(2,1)S(1)}, bf16[24,1024]{1,0:T(8,128)(2,1)S(1)}, u32[]{:S(2)}, u32[]{:S(2)}) %collective-permute-start.1) | collective-permute-done | bytes 49184 | tf_op jit(solution)/shard_map/ppermute | solution.py:21
  7.8 4.2 %shard_map.83 = (bf16[1,3584,512]{2,1,0:T(8,128)(2,1)S(1)}, bf16[1,3584,512]{2,1,0:T(8,128)(2,1)S(1)}, bf16[1,512,3584]{2,1,0:T(8,128)(2,1)S(1)}, f32[8,128]{1,0:T(8,128)S(1)}) custom-call(bf16[1,3584,512]{2,1,0:T(8,128)(2,1)} %refs_0_.1, bf16[1,3584,512]{2,1,0:T(8,128)(2,1)} %refs_1_.1, bf16[1,512,3584]{2,1,0:T(8,128)(2,1)} %refs_2_.1), custom_call_target="tpu_custom_call" | custom-call | bytes 22024192 | tf_op jit(solution)/shard_map/pallas_call | solution.py:44
  12.2 1.8 %collective-permute-start.11 = (bf16[24,3840]{1,0:T(8,128)(2,1)S(1)}, bf16[24,3840]{1,0:T(8,128)(2,1)S(1)}, u32[]{:S(2)}, u32[]{:S(2)}) collective-permute-start(bf16[24,3840]{1,0:T(8,128)(2,1)S(1)} %get-tuple-element.26.refs_0_), channel_id=1, source_target_pairs={{0,4},{1,11},{2,6},{3,9},{4,0},{5,15},{6,2},{7,13},{8,12},{9,3},{1... | collective-permute-start | bytes 552968 | tf_op jit(solution)/shard_map/ppermute | solution.py:21
  14.0 1.4 %collective-permute-start.12 = (bf16[24,3840]{1,0:T(8,128)(2,1)S(1)}, bf16[24,3840]{1,0:T(8,128)(2,1)S(1)}, u32[]{:S(2)}, u32[]{:S(2)}) collective-permute-start(bf16[24,3840]{1,0:T(8,128)(2,1)S(1)} %get-tuple-element.26.refs_0_), channel_id=1, source_target_pairs={{0,6},{1,9},{2,4},{3,11},{4,2},{5,13},{6,0},{7,15},{8,14},{9,1},{1... | collective-permute-start | bytes 552968 | tf_op jit(solution)/shard_map/ppermute | solution.py:21
  15.7 2.0 %collective-permute-done.11.refs_0_ = bf16[24,3840]{1,0:T(8,128)(2,1)S(1)} collective-permute-done((bf16[24,3840]{1,0:T(8,128)(2,1)S(1)}, bf16[24,3840]{1,0:T(8,128)(2,1)S(1)}, u32[]{:S(2)}, u32[]{:S(2)}) %collective-permute-start.11) | collective-permute-done | bytes 184352 | tf_op jit(solution)/shard_map/ppermute | solution.py:21
  18.1 3.2 %collective-permute-done.12.refs_1_ = bf16[24,3840]{1,0:T(8,128)(2,1)S(1)} collective-permute-done((bf16[24,3840]{1,0:T(8,128)(2,1)S(1)}, bf16[24,3840]{1,0:T(8,128)(2,1)S(1)}, u32[]{:S(2)}, u32[]{:S(2)}) %collective-permute-start.12) | collective-permute-done | bytes 184352 | tf_op jit(solution)/shard_map/ppermute | solution.py:21
  21.4 3.0 %collective-permute-start.5 = (bf16[24,1920]{1,0:T(8,128)(2,1)S(1)}, bf16[24,1920]{1,0:T(8,128)(2,1)S(1)}, u32[]{:S(2)}, u32[]{:S(2)}) collective-permute-start(bf16[24,1920]{1,0:T(8,128)(2,1)S(1)} %get-tuple-element.27), channel_id=1, source_target_pairs={{0,14},{1,15},{2,12},{3,13},{4,10},{5,11},{6,8},{7,9},{8,6},{9,7},... | collective-permute-start | bytes 276488 | tf_op jit(solution)/shard_map/ppermute | solution.py:21
  24.6 3.7 %collective-permute-done.5.refs_3_ = bf16[24,1920]{1,0:T(8,128)(2,1)S(1)} collective-permute-done((bf16[24,1920]{1,0:T(8,128)(2,1)S(1)}, bf16[24,1920]{1,0:T(8,128)(2,1)S(1)}, u32[]{:S(2)}, u32[]{:S(2)}) %collective-permute-start.5) | collective-permute-done | bytes 92192 | tf_op jit(solution)/shard_map/ppermute | solution.py:21
  28.3 1.9 %shard_map.87 = (f32[48,3584]{1,0:T(8,128)S(1)}, bf16[48,3584]{1,0:T(8,128)(2,1)S(1)}) custom-call(bf16[24,3840]{1,0:T(8,128)(2,1)S(1)} %collective-permute-done.11.refs_0_, bf16[24,3840]{1,0:T(8,128)(2,1)S(1)} %collective-permute-done.12.refs_1_, bf16[24,3840]{1,0:T(8,128)(2,1)S(1)} %collective-permute-done.13.refs_2_, ...), custom_call_target="tpu_custom_call" | custom-call | flops 1056964608 | bytes 12779520 | tf_op jit(solution)/shard_map/pallas_call | solution.py:44
  30.8 1.9 %shard_map.85 = (f32[48,3584]{1,0:T(8,128)S(1)}, bf16[24,3584]{1,0:T(8,128)(2,1)S(1)}, f32[24,1792]{1,0:T(8,128)S(1)}, bf16[24,1792]{1,0:T(8,128)(2,1)S(1)}) custom-call(bf16[24,3840]{1,0:T(8,128)(2,1)S(1)} %get-tuple-element.26.refs_0_, bf16[24,3840]{1,0:T(8,128)(2,1)S(1)} %collective-permute-done.3.refs_1_, ...), custom_call_target="tpu_custom_call" | custom-call | flops 1056964608 | bytes 12865536 | tf_op jit(solution)/shard_map/pallas_call | solution.py:44
  33.3 1.0 %collective-permute-done.8.refs_3_ = bf16[24,1792]{1,0:T(8,128)(2,1)S(1)} collective-permute-done((bf16[24,1792]{1,0:T(8,128)(2,1)S(1)}, bf16[24,1792]{1,0:T(8,128)(2,1)S(1)}, u32[]{:S(2)}, u32[]{:S(2)}) %collective-permute-start.8) | collective-permute-done | bytes 86048 | tf_op jit(solution)/shard_map/ppermute | solution.py:21
  34.4 2.5 %collective-permute-start.10 = (bf16[24,3584]{1,0:T(8,128)(2,1)S(1)}, bf16[24,3584]{1,0:T(8,128)(2,1)S(1)}, u32[]{:S(2)}, u32[]{:S(2)}) collective-permute-start(bf16[24,3584]{1,0:T(8,128)(2,1)S(1)} %get-tuple-element.36), channel_id=1, source_target_pairs={{0,2},{1,13},{2,0},{3,15},{4,6},{5,9},{6,4},{7,11},{8,10},{9,5},{1... | collective-permute-start | bytes 516104 | tf_op jit(solution)/shard_map/ppermute | solution.py:21
  36.9 0.8 %collective-permute-start.16 = (bf16[24,3584]{1,0:T(8,128)(2,1)S(1)}, bf16[24,3584]{1,0:T(8,128)(2,1)S(1)}, u32[]{:S(2)}, u32[]{:S(2)}) collective-permute-start(bf16[24,3584]{1,0:T(8,128)(2,1)S(1)} %get-tuple-element.39), channel_id=1, source_target_pairs={{0,4},{1,11},{2,6},{3,9},{4,0},{5,15},{6,2},{7,13},{8,12},{9,3},{1... | collective-permute-start | bytes 516104 | tf_op jit(solution)/shard_map/ppermute | solution.py:21
  37.7 0.8 %collective-permute-start.17 = (bf16[24,3584]{1,0:T(8,128)(2,1)S(1)}, bf16[24,3584]{1,0:T(8,128)(2,1)S(1)}, u32[]{:S(2)}, u32[]{:S(2)}) collective-permute-start(bf16[24,3584]{1,0:T(8,128)(2,1)S(1)} %get-tuple-element.40), channel_id=1, source_target_pairs={{0,6},{1,9},{2,4},{3,11},{4,2},{5,13},{6,0},{7,15},{8,14},{9,1},{1... | collective-permute-start | bytes 516104 | tf_op jit(solution)/shard_map/ppermute | solution.py:21
  38.5 2.5 %collective-permute-start.9 = (bf16[24,1792]{1,0:T(8,128)(2,1)S(1)}, bf16[24,1792]{1,0:T(8,128)(2,1)S(1)}, u32[]{:S(2)}, u32[]{:S(2)}) collective-permute-start(bf16[24,1792]{1,0:T(8,128)(2,1)S(1)} %get-tuple-element.35), channel_id=1, source_target_pairs={{0,14},{1,15},{2,12},{3,13},{4,10},{5,11},{6,8},{7,9},{8,6},{9,7},... | collective-permute-start | bytes 258056 | tf_op jit(solution)/shard_map/ppermute | solution.py:21
  41.0 4.7 %collective-permute-done.9.refs_1_ = bf16[24,1792]{1,0:T(8,128)(2,1)S(1)} collective-permute-done((bf16[24,1792]{1,0:T(8,128)(2,1)S(1)}, bf16[24,1792]{1,0:T(8,128)(2,1)S(1)}, u32[]{:S(2)}, u32[]{:S(2)}) %collective-permute-start.9) | collective-permute-done | bytes 86048 | tf_op jit(solution)/shard_map/ppermute | solution.py:21
  45.7 0.9 %collective-permute-done.17.refs_4_ = bf16[24,3584]{1,0:T(8,128)(2,1)S(1)} collective-permute-done((bf16[24,3584]{1,0:T(8,128)(2,1)S(1)}, bf16[24,3584]{1,0:T(8,128)(2,1)S(1)}, u32[]{:S(2)}, u32[]{:S(2)}) %collective-permute-start.17) | collective-permute-done | bytes 172064 | tf_op jit(solution)/shard_map/ppermute | solution.py:21
  46.8 0.8 %collective-permute-start.18 = (bf16[24,1792]{1,0:T(8,128)(2,1)S(1)}, bf16[24,1792]{1,0:T(8,128)(2,1)S(1)}, u32[]{:S(2)}, u32[]{:S(2)}) collective-permute-start(bf16[24,1792]{1,0:T(8,128)(2,1)S(1)} %get-tuple-element.42), channel_id=1, source_target_pairs={{0,1},{1,0},{2,3},{3,2},{4,5},{5,4},{6,7},{7,6},{8,9},{9,8},{10,11... | collective-permute-start | bytes 258056 | tf_op jit(solution)/shard_map/ppermute | solution.py:21
  47.6 0.9 %collective-permute-done.18.other_ref = bf16[24,1792]{1,0:T(8,128)(2,1)S(1)} collective-permute-done((bf16[24,1792]{1,0:T(8,128)(2,1)S(1)}, bf16[24,1792]{1,0:T(8,128)(2,1)S(1)}, u32[]{:S(2)}, u32[]{:S(2)}) %collective-permute-start.18) | collective-permute-done | bytes 86048 | tf_op jit(solution)/shard_map/ppermute | solution.py:21
  48.6 2.0 %collective-permute-start.19 = (bf16[24,896]{1,0:T(8,128)(2,1)S(1)}, bf16[24,896]{1,0:T(8,128)(2,1)S(1)}, u32[]{:S(2)}, u32[]{:S(2)}) collective-permute-start(bf16[24,896]{1,0:T(8,128)(2,1)S(1)} %get-tuple-element.44), channel_id=1, source_target_pairs={{0,16},{1,17},{2,18},{3,19},{4,20},{5,21},{6,22},{7,23},{8,24},{9,... | collective-permute-start | bytes 129032 | tf_op jit(solution)/shard_map/ppermute | solution.py:21
  50.6 3.0 %collective-permute-done.19.other_ref = bf16[24,896]{1,0:T(8,128)(2,1)S(1)} collective-permute-done((bf16[24,896]{1,0:T(8,128)(2,1)S(1)}, bf16[24,896]{1,0:T(8,128)(2,1)S(1)}, u32[]{:S(2)}, u32[]{:S(2)}) %collective-permute-start.19) | collective-permute-done | bytes 43040 | tf_op jit(solution)/shard_map/ppermute | solution.py:21
  53.6 0.6 %shard_map.91 = bf16[6,3584]{1,0:T(8,128)(2,1)} custom-call(f32[24,896]{1,0:T(8,128)S(1)} %get-tuple-element.43.near_ref, bf16[24,896]{1,0:T(8,128)(2,1)S(1)} %collective-permute-done.19.other_ref), custom_call_target="tpu_custom_call" | custom-call | bytes 172032 | tf_op jit(solution)/shard_map/pallas_call | solution.py:44
  (26 shorter events, 2.6 us)
Async XLA Ops:
  1.1 6.7 %collective-permute-start.1 = (bf16[24,1024]{1,0:T(8,128)(2,1)S(1)}, bf16[24,1024]{1,0:T(8,128)(2,1)S(1)}, u32[]{:S(2)}, u32[]{:S(2)}) collective-permute-start(bf16[24,1024]{1,0:T(8,128)(2,1)S(1)} %shard_map.82.own_ref), channel_id=1, source_target_pairs={{0,16},{1,17},{2,18},{3,19},{4,20},{5,21},{6,22},{7,23},{8,24},{9,... | collective-permute-start | bytes 147464 | tf_op jit(solution)/shard_map/ppermute | solution.py:21
  5.2 6.8 %collective-permute-start = (bf16[24,1024]{1,0:T(8,128)(2,1)S(1)}, bf16[24,1024]{1,0:T(8,128)(2,1)S(1)}, u32[]{:S(2)}, u32[]{:S(2)}) collective-permute-start(bf16[24,1024]{1,0:T(8,128)(2,1)S(1)} %shard_map.82.own_ref), channel_id=1, source_target_pairs={{0,1},{1,0},{2,3},{3,2},{4,5},{5,4},{6,7},{7,6},{8,9},{9,8},{10,11... | collective-permute-start | bytes 147464 | tf_op jit(solution)/shard_map/ppermute | solution.py:21
  7.8 4.3 %collective-permute-start.2 = (bf16[24,1024]{1,0:T(8,128)(2,1)S(1)}, bf16[24,1024]{1,0:T(8,128)(2,1)S(1)}, u32[]{:S(2)}, u32[]{:S(2)}) collective-permute-start(bf16[24,1024]{1,0:T(8,128)(2,1)S(1)} %collective-permute-done.1.far_ref), channel_id=1, source_target_pairs={{0,1},{1,0},{2,3},{3,2},{4,5},{5,4},{6,7},{7,6},{8,9},{9,8},{10,11... | collective-permute-start | bytes 147464 | tf_op jit(solution)/shard_map/ppermute | solution.py:21
  12.2 5.6 %collective-permute-start.11 = (bf16[24,3840]{1,0:T(8,128)(2,1)S(1)}, bf16[24,3840]{1,0:T(8,128)(2,1)S(1)}, u32[]{:S(2)}, u32[]{:S(2)}) collective-permute-start(bf16[24,3840]{1,0:T(8,128)(2,1)S(1)} %get-tuple-element.26.refs_0_), channel_id=1, source_target_pairs={{0,4},{1,11},{2,6},{3,9},{4,0},{5,15},{6,2},{7,13},{8,12},{9,3},{1... | collective-permute-start | bytes 552968 | tf_op jit(solution)/shard_map/ppermute | solution.py:21
  14.0 7.4 %collective-permute-start.12 = (bf16[24,3840]{1,0:T(8,128)(2,1)S(1)}, bf16[24,3840]{1,0:T(8,128)(2,1)S(1)}, u32[]{:S(2)}, u32[]{:S(2)}) collective-permute-start(bf16[24,3840]{1,0:T(8,128)(2,1)S(1)} %get-tuple-element.26.refs_0_), channel_id=1, source_target_pairs={{0,6},{1,9},{2,4},{3,11},{4,2},{5,13},{6,0},{7,15},{8,14},{9,1},{1... | collective-permute-start | bytes 552968 | tf_op jit(solution)/shard_map/ppermute | solution.py:21
  15.4 8.9 %collective-permute-start.3 = (bf16[24,3840]{1,0:T(8,128)(2,1)S(1)}, bf16[24,3840]{1,0:T(8,128)(2,1)S(1)}, u32[]{:S(2)}, u32[]{:S(2)}) collective-permute-start(bf16[24,3840]{1,0:T(8,128)(2,1)S(1)} %get-tuple-element.26.refs_0_), channel_id=1, source_target_pairs={{0,2},{1,13},{2,0},{3,15},{4,6},{5,9},{6,4},{7,11},{8,10},{9,5},{1... | collective-permute-start | bytes 552968 | tf_op jit(solution)/shard_map/ppermute | solution.py:21
  17.8 10.5 %collective-permute-start.13 = (bf16[24,3840]{1,0:T(8,128)(2,1)S(1)}, bf16[24,3840]{1,0:T(8,128)(2,1)S(1)}, u32[]{:S(2)}, u32[]{:S(2)}) collective-permute-start(bf16[24,3840]{1,0:T(8,128)(2,1)S(1)} %collective-permute-done.11.refs_0_), channel_id=1, source_target_pairs={{0,1},{1,0},{2,3},{3,2},{4,5},{5,4},{6,7},{7,6},{8,9},{9,8},{10,11... | collective-permute-start | bytes 552968 | tf_op jit(solution)/shard_map/ppermute | solution.py:21
  21.4 6.9 %collective-permute-start.14 = (bf16[24,3840]{1,0:T(8,128)(2,1)S(1)}, bf16[24,3840]{1,0:T(8,128)(2,1)S(1)}, u32[]{:S(2)}, u32[]{:S(2)}) collective-permute-start(bf16[24,3840]{1,0:T(8,128)(2,1)S(1)} %collective-permute-done.12.refs_1_), channel_id=1, source_target_pairs={{0,1},{1,0},{2,3},{3,2},{4,5},{5,4},{6,7},{7,6},{8,9},{9,8},{10,11... | collective-permute-start | bytes 552968 | tf_op jit(solution)/shard_map/ppermute | solution.py:21
  21.4 6.9 %collective-permute-start.5 = (bf16[24,1920]{1,0:T(8,128)(2,1)S(1)}, bf16[24,1920]{1,0:T(8,128)(2,1)S(1)}, u32[]{:S(2)}, u32[]{:S(2)}) collective-permute-start(bf16[24,1920]{1,0:T(8,128)(2,1)S(1)} %get-tuple-element.27), channel_id=1, source_target_pairs={{0,14},{1,15},{2,12},{3,13},{4,10},{5,11},{6,8},{7,9},{8,6},{9,7},... | collective-permute-start | bytes 276488 | tf_op jit(solution)/shard_map/ppermute | solution.py:21
  24.3 6.4 %collective-permute-start.4 = (bf16[24,3840]{1,0:T(8,128)(2,1)S(1)}, bf16[24,3840]{1,0:T(8,128)(2,1)S(1)}, u32[]{:S(2)}, u32[]{:S(2)}) collective-permute-start(bf16[24,3840]{1,0:T(8,128)(2,1)S(1)} %collective-permute-done.3.refs_1_), channel_id=1, source_target_pairs={{0,1},{1,0},{2,3},{3,2},{4,5},{5,4},{6,7},{7,6},{8,9},{9,8},{10,11... | collective-permute-start | bytes 552968 | tf_op jit(solution)/shard_map/ppermute | solution.py:21
  28.2 2.5 %collective-permute-start.6 = (bf16[24,1920]{1,0:T(8,128)(2,1)S(1)}, bf16[24,1920]{1,0:T(8,128)(2,1)S(1)}, u32[]{:S(2)}, u32[]{:S(2)}) collective-permute-start(bf16[24,1920]{1,0:T(8,128)(2,1)S(1)} %collective-permute-done.5.refs_3_), channel_id=1, source_target_pairs={{0,1},{1,0},{2,3},{3,2},{4,5},{5,4},{6,7},{7,6},{8,9},{9,8},{10,11... | collective-permute-start | bytes 276488 | tf_op jit(solution)/shard_map/ppermute | solution.py:21
  30.2 6.7 %collective-permute-start.15 = (bf16[48,3584]{1,0:T(8,128)(2,1)S(1)}, bf16[48,3584]{1,0:T(8,128)(2,1)S(1)}, u32[]{:S(2)}, u32[]{:S(2)}) collective-permute-start(bf16[48,3584]{1,0:T(8,128)(2,1)S(1)} %get-tuple-element.38), channel_id=1, source_target_pairs={{0,1},{1,0},{2,3},{3,2},{4,5},{5,4},{6,7},{7,6},{8,9},{9,8},{10,11... | collective-permute-start | bytes 1032200 | tf_op jit(solution)/shard_map/ppermute | solution.py:21
  32.7 1.6 %collective-permute-start.7 = (bf16[24,3584]{1,0:T(8,128)(2,1)S(1)}, bf16[24,3584]{1,0:T(8,128)(2,1)S(1)}, u32[]{:S(2)}, u32[]{:S(2)}) collective-permute-start(bf16[24,3584]{1,0:T(8,128)(2,1)S(1)} %get-tuple-element.32), channel_id=1, source_target_pairs={{0,1},{1,0},{2,3},{3,2},{4,5},{5,4},{6,7},{7,6},{8,9},{9,8},{10,11... | collective-permute-start | bytes 516104 | tf_op jit(solution)/shard_map/ppermute | solution.py:21
  32.8 1.5 %collective-permute-start.8 = (bf16[24,1792]{1,0:T(8,128)(2,1)S(1)}, bf16[24,1792]{1,0:T(8,128)(2,1)S(1)}, u32[]{:S(2)}, u32[]{:S(2)}) collective-permute-start(bf16[24,1792]{1,0:T(8,128)(2,1)S(1)} %get-tuple-element.34), channel_id=1, source_target_pairs={{0,1},{1,0},{2,3},{3,2},{4,5},{5,4},{6,7},{7,6},{8,9},{9,8},{10,11... | collective-permute-start | bytes 258056 | tf_op jit(solution)/shard_map/ppermute | solution.py:21
  34.4 11.3 %collective-permute-start.10 = (bf16[24,3584]{1,0:T(8,128)(2,1)S(1)}, bf16[24,3584]{1,0:T(8,128)(2,1)S(1)}, u32[]{:S(2)}, u32[]{:S(2)}) collective-permute-start(bf16[24,3584]{1,0:T(8,128)(2,1)S(1)} %get-tuple-element.36), channel_id=1, source_target_pairs={{0,2},{1,13},{2,0},{3,15},{4,6},{5,9},{6,4},{7,11},{8,10},{9,5},{1... | collective-permute-start | bytes 516104 | tf_op jit(solution)/shard_map/ppermute | solution.py:21
  36.9 8.8 %collective-permute-start.16 = (bf16[24,3584]{1,0:T(8,128)(2,1)S(1)}, bf16[24,3584]{1,0:T(8,128)(2,1)S(1)}, u32[]{:S(2)}, u32[]{:S(2)}) collective-permute-start(bf16[24,3584]{1,0:T(8,128)(2,1)S(1)} %get-tuple-element.39), channel_id=1, source_target_pairs={{0,4},{1,11},{2,6},{3,9},{4,0},{5,15},{6,2},{7,13},{8,12},{9,3},{1... | collective-permute-start | bytes 516104 | tf_op jit(solution)/shard_map/ppermute | solution.py:21
  37.7 8.9 %collective-permute-start.17 = (bf16[24,3584]{1,0:T(8,128)(2,1)S(1)}, bf16[24,3584]{1,0:T(8,128)(2,1)S(1)}, u32[]{:S(2)}, u32[]{:S(2)}) collective-permute-start(bf16[24,3584]{1,0:T(8,128)(2,1)S(1)} %get-tuple-element.40), channel_id=1, source_target_pairs={{0,6},{1,9},{2,4},{3,11},{4,2},{5,13},{6,0},{7,15},{8,14},{9,1},{1... | collective-permute-start | bytes 516104 | tf_op jit(solution)/shard_map/ppermute | solution.py:21
  38.5 7.2 %collective-permute-start.9 = (bf16[24,1792]{1,0:T(8,128)(2,1)S(1)}, bf16[24,1792]{1,0:T(8,128)(2,1)S(1)}, u32[]{:S(2)}, u32[]{:S(2)}) collective-permute-start(bf16[24,1792]{1,0:T(8,128)(2,1)S(1)} %get-tuple-element.35), channel_id=1, source_target_pairs={{0,14},{1,15},{2,12},{3,13},{4,10},{5,11},{6,8},{7,9},{8,6},{9,7},... | collective-permute-start | bytes 258056 | tf_op jit(solution)/shard_map/ppermute | solution.py:21
  46.8 1.8 %collective-permute-start.18 = (bf16[24,1792]{1,0:T(8,128)(2,1)S(1)}, bf16[24,1792]{1,0:T(8,128)(2,1)S(1)}, u32[]{:S(2)}, u32[]{:S(2)}) collective-permute-start(bf16[24,1792]{1,0:T(8,128)(2,1)S(1)} %get-tuple-element.42), channel_id=1, source_target_pairs={{0,1},{1,0},{2,3},{3,2},{4,5},{5,4},{6,7},{7,6},{8,9},{9,8},{10,11... | collective-permute-start | bytes 258056 | tf_op jit(solution)/shard_map/ppermute | solution.py:21
  48.6 5.0 %collective-permute-start.19 = (bf16[24,896]{1,0:T(8,128)(2,1)S(1)}, bf16[24,896]{1,0:T(8,128)(2,1)S(1)}, u32[]{:S(2)}, u32[]{:S(2)}) collective-permute-start(bf16[24,896]{1,0:T(8,128)(2,1)S(1)} %get-tuple-element.44), channel_id=1, source_target_pairs={{0,16},{1,17},{2,18},{3,19},{4,20},{5,21},{6,22},{7,23},{8,24},{9,... | collective-permute-start | bytes 129032 | tf_op jit(solution)/shard_map/ppermute | solution.py:21

commit v3 on v2

--- a/solution.py
+++ b/solution.py
@@ -1,3 +1,4 @@
+import functools
 import math
 
 import jax
@@ -204,55 +205,48 @@
 
 
 def fold_kernel(keep_ref, other_ref, *outs):
-    count = outs[0].shape[0]
+    rows, half = outs[0].shape
+    count = rows // 2
+    total = keep_ref[...] + wide(other_ref)
     for j, out_ref in enumerate(outs):
-        rows = slice(j * count, (j + 1) * count)
-        total = keep_ref[rows, :] + other_ref[rows, :].astype(jnp.float32)
-        out_ref[...] = total.astype(jnp.bfloat16)
-
-
-def sum_kernel(*refs):
+        part = total[j * count : (j + 1) * count]
+        both = jnp.concatenate([part[:, :half], part[:, half:]], axis=0)
+        out_ref[...] = both.astype(jnp.bfloat16)
+
+
+def sum_kernel(place, early, *refs):
     keep_ref, side_ref, *parts, mine_ref, give_ref = refs
-    rows, half = side_ref.shape
-    tokens = rows // 4
-    total = keep_ref[:rows, :]
-    for ref in parts:
+    count, half = side_ref.shape[0] // 2, side_ref.shape[1]
+    tokens = count // 2
+    piece = half // 2
+    rows = slice(place * count, (place + 1) * count)
+    total = keep_ref[rows, :]
+    for ref in parts[:early]:
+        total += wide(ref)[rows]
+    total = jnp.concatenate([total[:, :half], total[:, half:]], axis=0)
+    side = wide(side_ref)[rows]
+    total += jnp.concatenate(ordered(side, jnp.zeros_like(side)), axis=0)
+    for ref in parts[early:]:
         total += wide(ref)
-    side = wide(side_ref)
-    zero = jnp.zeros_like(side)
-    total += jnp.concatenate(ordered(side, zero), axis=1)
-    near = ordered(total[:tokens], total[tokens : 2 * tokens])
-    far = ordered(total[2 * tokens : 3 * tokens], total[3 * tokens :])
+    quarters = [total[q * tokens : (q + 1) * tokens] for q in range(4)]
+    pairs = [ordered(quarters[0], quarters[1]), ordered(quarters[2], quarters[3])]
 
     def folded(which):
-        columns = (slice(0, half), slice(half, 2 * half))
-        return jnp.concatenate([b[which][:, c] for c in columns for b in (near, far)], axis=0)
+        pieces = [pair[which][:, c : c + piece] for pair in pairs for c in (0, piece)]
+        return jnp.concatenate(pieces, axis=0)
 
     mine_ref[...] = folded(0)
     give_ref[...] = folded(1).astype(jnp.bfloat16)
 
 
-def split_kernel(mine_ref, other_ref, near_ref, far_ref):
-    total = mine_ref[...] + wide(other_ref)
-    tokens = total.shape[0] // 4
-    piece = near_ref.shape[1]
-
-    def folded(which):
-        pieces = []
-        for side in range(2):
-            start = (2 * side + which) * tokens
-            rows = total[start : start + tokens]
-            pieces += [rows[:, :piece], rows[:, piece:]]
-        return jnp.concatenate(pieces, axis=0)
-
-    near_ref[...] = folded(0)
-    far_ref[...] = folded(1).astype(jnp.bfloat16)
-
-
-def finish_kernel(near_ref, other_ref, out_ref):
+def add_kernel(mine_ref, other_ref, out_ref):
+    out_ref[...] = (mine_ref[...] + wide(other_ref)).astype(out_ref.dtype)
+
+
+def finish_kernel(near_ref, beside_ref, other_ref, out_ref):
     tokens, width = out_ref.shape
     piece = width // PARTS
-    total = near_ref[...] + wide(other_ref)
+    total = near_ref[...] + wide(beside_ref) + wide(other_ref)
     for p in range(PARTS):
         rows = total[p * tokens : (p + 1) * tokens]
         out_ref[:, p * piece : (p + 1) * piece] = rows.astype(jnp.bfloat16)
@@ -350,28 +344,32 @@
         *loaded,
         flops=6 * late * work,
     )
-    parts = call(
-        fold_kernel, [shape((rows, width), bf16)] * late, 8 * MIB, late_keep, swapped(late_give, 1)
-    )
-    parts = [*first_parts, *parts]
+    folded = call(
+        fold_kernel,
+        [shape((rows, half), bf16)] * (2 * late),
+        8 * MIB,
+        late_keep,
+        swapped(late_give, 1),
+    )
     side = swapped(side, shared)
-    parts = [swapped(part, *step) for part, step in zip(parts, steps)]
-    mine, give = call(
-        sum_kernel,
-        [shape((rows, half), f32), shape((rows, half), bf16)],
-        8 * MIB,
-        keep,
-        side,
-        *parts,
-    )
-    near, give = call(
-        split_kernel,
-        [shape((PARTS * tokens, piece), f32), shape((PARTS * tokens, piece), bf16)],
-        4 * MIB,
-        mine,
-        swapped(give, 1),
-    )
-    return call(finish_kernel, [shape((tokens, width), bf16)], 4 * MIB, near, swapped(give, far))
+    first_parts = [swapped(part, *step) for part, step in zip(first_parts, steps)]
+
+    def summed(place):
+        parts = [swapped(part, *step) for part, step in zip(folded[place::2], steps[early:])]
+        mine, give = call(
+            functools.partial(sum_kernel, place, early),
+            [shape((rows, piece), f32), shape((rows, piece), bf16)],
+            8 * MIB,
+            keep,
+            side,
+            *first_parts,
+            *parts,
+        )
+        return mine, swapped(give, 1)
+
+    distant = call(add_kernel, [shape((rows, piece), bf16)], 4 * MIB, *summed(1))
+    distant = swapped(distant, far)
+    return call(finish_kernel, [shape((tokens, width), bf16)], 4 * MIB, *summed(0), distant)
 
 
 def early_count(devices):

time: 54.4 us -> 55.6 us (1.022)
  starting transfers between devices: 21.9 us -> 22.6 us
    ppermute x20 -> x23, starting transfers between devices: 21.9 us -> 22.6 us  [swapped(): return lax.ppermute(array, 'ep', pairs)]
    ppermute x20 -> x23, waiting for transfers between devices: 22 us -> 22.4 us  [swapped(): return lax.ppermute(array, 'ep', pairs)]
    pallas_call x10 -> x11, Pallas kernels: 10.3 us -> 10.3 us  [call(): pl.pallas_call(kernel, out_shape=outs[0] if single else tuple(outs), in_s...]
  transfers between devices with their start and end apart: 20 -> 23, of which waited for: 9 -> 10; matrix products, arithmetic and copies ran while one was open for 0% -> 0% of each run, Pallas kernels for 15% -> 15%
where the time goes in v3:
time: 55.6 us; the launch traced here: 55.4 us
  starting transfers between devices  22.6 us (41%)
  waiting for transfers between devices  22.4 us (40%)
  Pallas kernels  10.3 us (19%)
    ppermute x23, starting transfers between devices, swapped(): return lax.ppermute(array, 'ep', pairs)  22.6 us
    ppermute x23, waiting for transfers between devices, swapped(): return lax.ppermute(array, 'ep', pairs)  22.4 us
    pallas_call x11, Pallas kernels, call(): pl.pallas_call(kernel, out_shape=outs[0] if single else tuple(outs), in_s...  10.3 us
  transfers between devices with their start and end apart: 23, of which 10 were waited for; matrix products, arithmetic and copies ran while one was open for 0% of the time, Pallas kernels for 15%

profile of v3, /device:TPU:0, one launch (start us, length us, event | category | flops | bytes accessed | tf_op | source)
XLA Modules:
  0.0 55.4 jit_solution(6386133505839703947)
XLA Ops:
  0.0 1.1 %shard_map.82.own_ref = bf16[24,1024]{1,0:T(8,128)(2,1)S(1)} custom-call(s32[2]{0:T(128)} %draft_hbm.1, bf16[6,3584]{1,0:T(8,128)(2,1)} %states_hbm.1, f32[3584]{0:T(1024)} %gain_hbm.1, f32[6,8]{1,0:T(8,128)} %scores_hbm.1, s32[6,8]{1,0:T(8,128)} %routes_hbm.1), custom_call_target="tpu_custom_call" | custom-call | bytes 106888 | tf_op jit(solution)/shard_map/pallas_call | solution.py:45
  1.1 4.1 %collective-permute-start.1 = (bf16[24,1024]{1,0:T(8,128)(2,1)S(1)}, bf16[24,1024]{1,0:T(8,128)(2,1)S(1)}, u32[]{:S(2)}, u32[]{:S(2)}) collective-permute-start(bf16[24,1024]{1,0:T(8,128)(2,1)S(1)} %shard_map.82.own_ref), channel_id=1, source_target_pairs={{0,16},{1,17},{2,18},{3,19},{4,20},{5,21},{6,22},{7,23},{8,24},{9,... | collective-permute-start | bytes 147464 | tf_op jit(solution)/shard_map/ppermute | solution.py:22
  5.2 2.6 %collective-permute-done.1.far_ref = bf16[24,1024]{1,0:T(8,128)(2,1)S(1)} collective-permute-done((bf16[24,1024]{1,0:T(8,128)(2,1)S(1)}, bf16[24,1024]{1,0:T(8,128)(2,1)S(1)}, u32[]{:S(2)}, u32[]{:S(2)}) %collective-permute-start.1) | collective-permute-done | bytes 49184 | tf_op jit(solution)/shard_map/ppermute | solution.py:22
  7.8 4.2 %shard_map.83 = (bf16[1,3584,512]{2,1,0:T(8,128)(2,1)S(1)}, bf16[1,3584,512]{2,1,0:T(8,128)(2,1)S(1)}, bf16[1,512,3584]{2,1,0:T(8,128)(2,1)S(1)}, f32[8,128]{1,0:T(8,128)S(1)}) custom-call(bf16[1,3584,512]{2,1,0:T(8,128)(2,1)} %refs_0_.1, bf16[1,3584,512]{2,1,0:T(8,128)(2,1)} %refs_1_.1, bf16[1,512,3584]{2,1,0:T(8,128)(2,1)} %refs_2_.1), custom_call_target="tpu_custom_call" | custom-call | bytes 22024192 | tf_op jit(solution)/shard_map/pallas_call | solution.py:45
  12.2 1.8 %collective-permute-start.11 = (bf16[24,3840]{1,0:T(8,128)(2,1)S(1)}, bf16[24,3840]{1,0:T(8,128)(2,1)S(1)}, u32[]{:S(2)}, u32[]{:S(2)}) collective-permute-start(bf16[24,3840]{1,0:T(8,128)(2,1)S(1)} %get-tuple-element.28.refs_0_), channel_id=1, source_target_pairs={{0,4},{1,11},{2,6},{3,9},{4,0},{5,15},{6,2},{7,13},{8,12},{9,3},{1... | collective-permute-start | bytes 552968 | tf_op jit(solution)/shard_map/ppermute | solution.py:22
  14.0 1.4 %collective-permute-start.12 = (bf16[24,3840]{1,0:T(8,128)(2,1)S(1)}, bf16[24,3840]{1,0:T(8,128)(2,1)S(1)}, u32[]{:S(2)}, u32[]{:S(2)}) collective-permute-start(bf16[24,3840]{1,0:T(8,128)(2,1)S(1)} %get-tuple-element.28.refs_0_), channel_id=1, source_target_pairs={{0,6},{1,9},{2,4},{3,11},{4,2},{5,13},{6,0},{7,15},{8,14},{9,1},{1... | collective-permute-start | bytes 552968 | tf_op jit(solution)/shard_map/ppermute | solution.py:22
  15.7 2.0 %collective-permute-done.11.refs_0_ = bf16[24,3840]{1,0:T(8,128)(2,1)S(1)} collective-permute-done((bf16[24,3840]{1,0:T(8,128)(2,1)S(1)}, bf16[24,3840]{1,0:T(8,128)(2,1)S(1)}, u32[]{:S(2)}, u32[]{:S(2)}) %collective-permute-start.11) | collective-permute-done | bytes 184352 | tf_op jit(solution)/shard_map/ppermute | solution.py:22
  18.1 3.2 %collective-permute-done.12.refs_1_ = bf16[24,3840]{1,0:T(8,128)(2,1)S(1)} collective-permute-done((bf16[24,3840]{1,0:T(8,128)(2,1)S(1)}, bf16[24,3840]{1,0:T(8,128)(2,1)S(1)}, u32[]{:S(2)}, u32[]{:S(2)}) %collective-permute-start.12) | collective-permute-done | bytes 184352 | tf_op jit(solution)/shard_map/ppermute | solution.py:22
  21.4 3.0 %collective-permute-start.5 = (bf16[24,1920]{1,0:T(8,128)(2,1)S(1)}, bf16[24,1920]{1,0:T(8,128)(2,1)S(1)}, u32[]{:S(2)}, u32[]{:S(2)}) collective-permute-start(bf16[24,1920]{1,0:T(8,128)(2,1)S(1)} %get-tuple-element.29), channel_id=1, source_target_pairs={{0,14},{1,15},{2,12},{3,13},{4,10},{5,11},{6,8},{7,9},{8,6},{9,7},... | collective-permute-start | bytes 276488 | tf_op jit(solution)/shard_map/ppermute | solution.py:22
  24.6 3.7 %collective-permute-done.5.refs_3_ = bf16[24,1920]{1,0:T(8,128)(2,1)S(1)} collective-permute-done((bf16[24,1920]{1,0:T(8,128)(2,1)S(1)}, bf16[24,1920]{1,0:T(8,128)(2,1)S(1)}, u32[]{:S(2)}, u32[]{:S(2)}) %collective-permute-start.5) | collective-permute-done | bytes 92192 | tf_op jit(solution)/shard_map/ppermute | solution.py:22
  28.3 1.9 %shard_map.87 = (f32[48,3584]{1,0:T(8,128)S(1)}, bf16[48,3584]{1,0:T(8,128)(2,1)S(1)}) custom-call(bf16[24,3840]{1,0:T(8,128)(2,1)S(1)} %collective-permute-done.11.refs_0_, bf16[24,3840]{1,0:T(8,128)(2,1)S(1)} %collective-permute-done.12.refs_1_, bf16[24,3840]{1,0:T(8,128)(2,1)S(1)} %collective-permute-done.13.refs_2_, ...), custom_call_target="tpu_custom_call" | custom-call | flops 1056964608 | bytes 12779520 | tf_op jit(solution)/shard_map/pallas_call | solution.py:45
  30.8 1.9 %shard_map.85 = (f32[48,3584]{1,0:T(8,128)S(1)}, bf16[24,3584]{1,0:T(8,128)(2,1)S(1)}, f32[24,1792]{1,0:T(8,128)S(1)}, bf16[24,1792]{1,0:T(8,128)(2,1)S(1)}) custom-call(bf16[24,3840]{1,0:T(8,128)(2,1)S(1)} %get-tuple-element.28.refs_0_, bf16[24,3840]{1,0:T(8,128)(2,1)S(1)} %collective-permute-done.3.refs_1_, ...), custom_call_target="tpu_custom_call" | custom-call | flops 1056964608 | bytes 12865536 | tf_op jit(solution)/shard_map/pallas_call | solution.py:45
  33.3 1.0 %collective-permute-done.8.refs_3_ = bf16[24,1792]{1,0:T(8,128)(2,1)S(1)} collective-permute-done((bf16[24,1792]{1,0:T(8,128)(2,1)S(1)}, bf16[24,1792]{1,0:T(8,128)(2,1)S(1)}, u32[]{:S(2)}, u32[]{:S(2)}) %collective-permute-start.8) | collective-permute-done | bytes 86048 | tf_op jit(solution)/shard_map/ppermute | solution.py:22
  34.4 2.5 %collective-permute-start.10 = (bf16[24,3584]{1,0:T(8,128)(2,1)S(1)}, bf16[24,3584]{1,0:T(8,128)(2,1)S(1)}, u32[]{:S(2)}, u32[]{:S(2)}) collective-permute-start(bf16[24,3584]{1,0:T(8,128)(2,1)S(1)} %get-tuple-element.38), channel_id=1, source_target_pairs={{0,2},{1,13},{2,0},{3,15},{4,6},{5,9},{6,4},{7,11},{8,10},{9,5},{1... | collective-permute-start | bytes 516104 | tf_op jit(solution)/shard_map/ppermute | solution.py:22
  36.9 0.6 %collective-permute-start.9 = (bf16[24,1792]{1,0:T(8,128)(2,1)S(1)}, bf16[24,1792]{1,0:T(8,128)(2,1)S(1)}, u32[]{:S(2)}, u32[]{:S(2)}) collective-permute-start(bf16[24,1792]{1,0:T(8,128)(2,1)S(1)} %get-tuple-element.37), channel_id=1, source_target_pairs={{0,14},{1,15},{2,12},{3,13},{4,10},{5,11},{6,8},{7,9},{8,6},{9,7},... | collective-permute-start | bytes 258056 | tf_op jit(solution)/shard_map/ppermute | solution.py:22
  37.6 1.6 %collective-permute-start.19 = (bf16[24,1792]{1,0:T(8,128)(2,1)S(1)}, bf16[24,1792]{1,0:T(8,128)(2,1)S(1)}, u32[]{:S(2)}, u32[]{:S(2)}) collective-permute-start(bf16[24,1792]{1,0:T(8,128)(2,1)S(1)} %get-tuple-element.45), channel_id=1, source_target_pairs={{0,4},{1,11},{2,6},{3,9},{4,0},{5,15},{6,2},{7,13},{8,12},{9,3},{1... | collective-permute-start | bytes 258056 | tf_op jit(solution)/shard_map/ppermute | solution.py:22
  39.2 1.9 %collective-permute-start.20 = (bf16[24,1792]{1,0:T(8,128)(2,1)S(1)}, bf16[24,1792]{1,0:T(8,128)(2,1)S(1)}, u32[]{:S(2)}, u32[]{:S(2)}) collective-permute-start(bf16[24,1792]{1,0:T(8,128)(2,1)S(1)} %get-tuple-element.46), channel_id=1, source_target_pairs={{0,6},{1,9},{2,4},{3,11},{4,2},{5,13},{6,0},{7,15},{8,14},{9,1},{1... | collective-permute-start | bytes 258056 | tf_op jit(solution)/shard_map/ppermute | solution.py:22
  41.0 1.5 %collective-permute-start.16 = (bf16[24,1792]{1,0:T(8,128)(2,1)S(1)}, bf16[24,1792]{1,0:T(8,128)(2,1)S(1)}, u32[]{:S(2)}, u32[]{:S(2)}) collective-permute-start(bf16[24,1792]{1,0:T(8,128)(2,1)S(1)} %get-tuple-element.41), channel_id=1, source_target_pairs={{0,4},{1,11},{2,6},{3,9},{4,0},{5,15},{6,2},{7,13},{8,12},{9,3},{1... | collective-permute-start | bytes 258056 | tf_op jit(solution)/shard_map/ppermute | solution.py:22
  42.6 1.6 %collective-permute-done.9.refs_1_ = bf16[24,1792]{1,0:T(8,128)(2,1)S(1)} collective-permute-done((bf16[24,1792]{1,0:T(8,128)(2,1)S(1)}, bf16[24,1792]{1,0:T(8,128)(2,1)S(1)}, u32[]{:S(2)}, u32[]{:S(2)}) %collective-permute-start.9) | collective-permute-done | bytes 86048 | tf_op jit(solution)/shard_map/ppermute | solution.py:22
  44.2 1.5 %collective-permute-done.20.refs_4_ = bf16[24,1792]{1,0:T(8,128)(2,1)S(1)} collective-permute-done((bf16[24,1792]{1,0:T(8,128)(2,1)S(1)}, bf16[24,1792]{1,0:T(8,128)(2,1)S(1)}, u32[]{:S(2)}, u32[]{:S(2)}) %collective-permute-start.20) | collective-permute-done | bytes 86048 | tf_op jit(solution)/shard_map/ppermute | solution.py:22
  46.4 3.2 %collective-permute-done.17.refs_4_ = bf16[24,1792]{1,0:T(8,128)(2,1)S(1)} collective-permute-done((bf16[24,1792]{1,0:T(8,128)(2,1)S(1)}, bf16[24,1792]{1,0:T(8,128)(2,1)S(1)}, u32[]{:S(2)}, u32[]{:S(2)}) %collective-permute-start.17) | collective-permute-done | bytes 86048 | tf_op jit(solution)/shard_map/ppermute | solution.py:22
  49.8 2.0 %collective-permute-start.22 = (bf16[24,896]{1,0:T(8,128)(2,1)S(1)}, bf16[24,896]{1,0:T(8,128)(2,1)S(1)}, u32[]{:S(2)}, u32[]{:S(2)}) collective-permute-start(bf16[24,896]{1,0:T(8,128)(2,1)S(1)} %shard_map.91), channel_id=1, source_target_pairs={{0,16},{1,17},{2,18},{3,19},{4,20},{5,21},{6,22},{7,23},{8,24},{9,... | collective-permute-start | bytes 129032 | tf_op jit(solution)/shard_map/ppermute | solution.py:22
  51.7 3.0 %collective-permute-done.22.other_ref = bf16[24,896]{1,0:T(8,128)(2,1)S(1)} collective-permute-done((bf16[24,896]{1,0:T(8,128)(2,1)S(1)}, bf16[24,896]{1,0:T(8,128)(2,1)S(1)}, u32[]{:S(2)}, u32[]{:S(2)}) %collective-permute-start.22) | collective-permute-done | bytes 43040 | tf_op jit(solution)/shard_map/ppermute | solution.py:22
  54.8 0.6 %shard_map.92 = bf16[6,3584]{1,0:T(8,128)(2,1)} custom-call(f32[24,896]{1,0:T(8,128)S(1)} %get-tuple-element.43.near_ref, bf16[24,896]{1,0:T(8,128)(2,1)S(1)} %collective-permute-done.18.beside_ref, bf16[24,896]{1,0:T(8,128)(2,1)S(1)} %collective-permute-done.22.other_ref), custom_call_target="tpu_custom_call" | custom-call | bytes 215040 | tf_op jit(solution)/shard_map/pallas_call | solution.py:45
  (33 shorter events, 3.3 us)
Async XLA Ops:
  1.1 6.7 %collective-permute-start.1 = (bf16[24,1024]{1,0:T(8,128)(2,1)S(1)}, bf16[24,1024]{1,0:T(8,128)(2,1)S(1)}, u32[]{:S(2)}, u32[]{:S(2)}) collective-permute-start(bf16[24,1024]{1,0:T(8,128)(2,1)S(1)} %shard_map.82.own_ref), channel_id=1, source_target_pairs={{0,16},{1,17},{2,18},{3,19},{4,20},{5,21},{6,22},{7,23},{8,24},{9,... | collective-permute-start | bytes 147464 | tf_op jit(solution)/shard_map/ppermute | solution.py:22
  5.2 6.8 %collective-permute-start = (bf16[24,1024]{1,0:T(8,128)(2,1)S(1)}, bf16[24,1024]{1,0:T(8,128)(2,1)S(1)}, u32[]{:S(2)}, u32[]{:S(2)}) collective-permute-start(bf16[24,1024]{1,0:T(8,128)(2,1)S(1)} %shard_map.82.own_ref), channel_id=1, source_target_pairs={{0,1},{1,0},{2,3},{3,2},{4,5},{5,4},{6,7},{7,6},{8,9},{9,8},{10,11... | collective-permute-start | bytes 147464 | tf_op jit(solution)/shard_map/ppermute | solution.py:22
  7.8 4.3 %collective-permute-start.2 = (bf16[24,1024]{1,0:T(8,128)(2,1)S(1)}, bf16[24,1024]{1,0:T(8,128)(2,1)S(1)}, u32[]{:S(2)}, u32[]{:S(2)}) collective-permute-start(bf16[24,1024]{1,0:T(8,128)(2,1)S(1)} %collective-permute-done.1.far_ref), channel_id=1, source_target_pairs={{0,1},{1,0},{2,3},{3,2},{4,5},{5,4},{6,7},{7,6},{8,9},{9,8},{10,11... | collective-permute-start | bytes 147464 | tf_op jit(solution)/shard_map/ppermute | solution.py:22
  12.2 5.6 %collective-permute-start.11 = (bf16[24,3840]{1,0:T(8,128)(2,1)S(1)}, bf16[24,3840]{1,0:T(8,128)(2,1)S(1)}, u32[]{:S(2)}, u32[]{:S(2)}) collective-permute-start(bf16[24,3840]{1,0:T(8,128)(2,1)S(1)} %get-tuple-element.28.refs_0_), channel_id=1, source_target_pairs={{0,4},{1,11},{2,6},{3,9},{4,0},{5,15},{6,2},{7,13},{8,12},{9,3},{1... | collective-permute-start | bytes 552968 | tf_op jit(solution)/shard_map/ppermute | solution.py:22
  14.0 7.4 %collective-permute-start.12 = (bf16[24,3840]{1,0:T(8,128)(2,1)S(1)}, bf16[24,3840]{1,0:T(8,128)(2,1)S(1)}, u32[]{:S(2)}, u32[]{:S(2)}) collective-permute-start(bf16[24,3840]{1,0:T(8,128)(2,1)S(1)} %get-tuple-element.28.refs_0_), channel_id=1, source_target_pairs={{0,6},{1,9},{2,4},{3,11},{4,2},{5,13},{6,0},{7,15},{8,14},{9,1},{1... | collective-permute-start | bytes 552968 | tf_op jit(solution)/shard_map/ppermute | solution.py:22
  15.4 8.9 %collective-permute-start.3 = (bf16[24,3840]{1,0:T(8,128)(2,1)S(1)}, bf16[24,3840]{1,0:T(8,128)(2,1)S(1)}, u32[]{:S(2)}, u32[]{:S(2)}) collective-permute-start(bf16[24,3840]{1,0:T(8,128)(2,1)S(1)} %get-tuple-element.28.refs_0_), channel_id=1, source_target_pairs={{0,2},{1,13},{2,0},{3,15},{4,6},{5,9},{6,4},{7,11},{8,10},{9,5},{1... | collective-permute-start | bytes 552968 | tf_op jit(solution)/shard_map/ppermute | solution.py:22
  17.8 10.5 %collective-permute-start.13 = (bf16[24,3840]{1,0:T(8,128)(2,1)S(1)}, bf16[24,3840]{1,0:T(8,128)(2,1)S(1)}, u32[]{:S(2)}, u32[]{:S(2)}) collective-permute-start(bf16[24,3840]{1,0:T(8,128)(2,1)S(1)} %collective-permute-done.11.refs_0_), channel_id=1, source_target_pairs={{0,1},{1,0},{2,3},{3,2},{4,5},{5,4},{6,7},{7,6},{8,9},{9,8},{10,11... | collective-permute-start | bytes 552968 | tf_op jit(solution)/shard_map/ppermute | solution.py:22
  21.4 6.9 %collective-permute-start.14 = (bf16[24,3840]{1,0:T(8,128)(2,1)S(1)}, bf16[24,3840]{1,0:T(8,128)(2,1)S(1)}, u32[]{:S(2)}, u32[]{:S(2)}) collective-permute-start(bf16[24,3840]{1,0:T(8,128)(2,1)S(1)} %collective-permute-done.12.refs_1_), channel_id=1, source_target_pairs={{0,1},{1,0},{2,3},{3,2},{4,5},{5,4},{6,7},{7,6},{8,9},{9,8},{10,11... | collective-permute-start | bytes 552968 | tf_op jit(solution)/shard_map/ppermute | solution.py:22
  21.4 6.9 %collective-permute-start.5 = (bf16[24,1920]{1,0:T(8,128)(2,1)S(1)}, bf16[24,1920]{1,0:T(8,128)(2,1)S(1)}, u32[]{:S(2)}, u32[]{:S(2)}) collective-permute-start(bf16[24,1920]{1,0:T(8,128)(2,1)S(1)} %get-tuple-element.29), channel_id=1, source_target_pairs={{0,14},{1,15},{2,12},{3,13},{4,10},{5,11},{6,8},{7,9},{8,6},{9,7},... | collective-permute-start | bytes 276488 | tf_op jit(solution)/shard_map/ppermute | solution.py:22
  24.3 6.4 %collective-permute-start.4 = (bf16[24,3840]{1,0:T(8,128)(2,1)S(1)}, bf16[24,3840]{1,0:T(8,128)(2,1)S(1)}, u32[]{:S(2)}, u32[]{:S(2)}) collective-permute-start(bf16[24,3840]{1,0:T(8,128)(2,1)S(1)} %collective-permute-done.3.refs_1_), channel_id=1, source_target_pairs={{0,1},{1,0},{2,3},{3,2},{4,5},{5,4},{6,7},{7,6},{8,9},{9,8},{10,11... | collective-permute-start | bytes 552968 | tf_op jit(solution)/shard_map/ppermute | solution.py:22
  28.2 2.5 %collective-permute-start.6 = (bf16[24,1920]{1,0:T(8,128)(2,1)S(1)}, bf16[24,1920]{1,0:T(8,128)(2,1)S(1)}, u32[]{:S(2)}, u32[]{:S(2)}) collective-permute-start(bf16[24,1920]{1,0:T(8,128)(2,1)S(1)} %collective-permute-done.5.refs_3_), channel_id=1, source_target_pairs={{0,1},{1,0},{2,3},{3,2},{4,5},{5,4},{6,7},{7,6},{8,9},{9,8},{10,11... | collective-permute-start | bytes 276488 | tf_op jit(solution)/shard_map/ppermute | solution.py:22
  30.2 7.3 %collective-permute-start.15 = (bf16[48,3584]{1,0:T(8,128)(2,1)S(1)}, bf16[48,3584]{1,0:T(8,128)(2,1)S(1)}, u32[]{:S(2)}, u32[]{:S(2)}) collective-permute-start(bf16[48,3584]{1,0:T(8,128)(2,1)S(1)} %get-tuple-element.40), channel_id=1, source_target_pairs={{0,1},{1,0},{2,3},{3,2},{4,5},{5,4},{6,7},{7,6},{8,9},{9,8},{10,11... | collective-permute-start | bytes 1032200 | tf_op jit(solution)/shard_map/ppermute | solution.py:22
  32.7 1.6 %collective-permute-start.7 = (bf16[24,3584]{1,0:T(8,128)(2,1)S(1)}, bf16[24,3584]{1,0:T(8,128)(2,1)S(1)}, u32[]{:S(2)}, u32[]{:S(2)}) collective-permute-start(bf16[24,3584]{1,0:T(8,128)(2,1)S(1)} %get-tuple-element.34), channel_id=1, source_target_pairs={{0,1},{1,0},{2,3},{3,2},{4,5},{5,4},{6,7},{7,6},{8,9},{9,8},{10,11... | collective-permute-start | bytes 516104 | tf_op jit(solution)/shard_map/ppermute | solution.py:22
  32.8 1.5 %collective-permute-start.8 = (bf16[24,1792]{1,0:T(8,128)(2,1)S(1)}, bf16[24,1792]{1,0:T(8,128)(2,1)S(1)}, u32[]{:S(2)}, u32[]{:S(2)}) collective-permute-start(bf16[24,1792]{1,0:T(8,128)(2,1)S(1)} %get-tuple-element.36), channel_id=1, source_target_pairs={{0,1},{1,0},{2,3},{3,2},{4,5},{5,4},{6,7},{7,6},{8,9},{9,8},{10,11... | collective-permute-start | bytes 258056 | tf_op jit(solution)/shard_map/ppermute | solution.py:22
  34.4 9.8 %collective-permute-start.10 = (bf16[24,3584]{1,0:T(8,128)(2,1)S(1)}, bf16[24,3584]{1,0:T(8,128)(2,1)S(1)}, u32[]{:S(2)}, u32[]{:S(2)}) collective-permute-start(bf16[24,3584]{1,0:T(8,128)(2,1)S(1)} %get-tuple-element.38), channel_id=1, source_target_pairs={{0,2},{1,13},{2,0},{3,15},{4,6},{5,9},{6,4},{7,11},{8,10},{9,5},{1... | collective-permute-start | bytes 516104 | tf_op jit(solution)/shard_map/ppermute | solution.py:22
  36.9 7.3 %collective-permute-start.9 = (bf16[24,1792]{1,0:T(8,128)(2,1)S(1)}, bf16[24,1792]{1,0:T(8,128)(2,1)S(1)}, u32[]{:S(2)}, u32[]{:S(2)}) collective-permute-start(bf16[24,1792]{1,0:T(8,128)(2,1)S(1)} %get-tuple-element.37), channel_id=1, source_target_pairs={{0,14},{1,15},{2,12},{3,13},{4,10},{5,11},{6,8},{7,9},{8,6},{9,7},... | collective-permute-start | bytes 258056 | tf_op jit(solution)/shard_map/ppermute | solution.py:22
  37.6 6.6 %collective-permute-start.19 = (bf16[24,1792]{1,0:T(8,128)(2,1)S(1)}, bf16[24,1792]{1,0:T(8,128)(2,1)S(1)}, u32[]{:S(2)}, u32[]{:S(2)}) collective-permute-start(bf16[24,1792]{1,0:T(8,128)(2,1)S(1)} %get-tuple-element.45), channel_id=1, source_target_pairs={{0,4},{1,11},{2,6},{3,9},{4,0},{5,15},{6,2},{7,13},{8,12},{9,3},{1... | collective-permute-start | bytes 258056 | tf_op jit(solution)/shard_map/ppermute | solution.py:22
  39.2 6.5 %collective-permute-start.20 = (bf16[24,1792]{1,0:T(8,128)(2,1)S(1)}, bf16[24,1792]{1,0:T(8,128)(2,1)S(1)}, u32[]{:S(2)}, u32[]{:S(2)}) collective-permute-start(bf16[24,1792]{1,0:T(8,128)(2,1)S(1)} %get-tuple-element.46), channel_id=1, source_target_pairs={{0,6},{1,9},{2,4},{3,11},{4,2},{5,13},{6,0},{7,15},{8,14},{9,1},{1... | collective-permute-start | bytes 258056 | tf_op jit(solution)/shard_map/ppermute | solution.py:22
  41.0 5.3 %collective-permute-start.16 = (bf16[24,1792]{1,0:T(8,128)(2,1)S(1)}, bf16[24,1792]{1,0:T(8,128)(2,1)S(1)}, u32[]{:S(2)}, u32[]{:S(2)}) collective-permute-start(bf16[24,1792]{1,0:T(8,128)(2,1)S(1)} %get-tuple-element.41), channel_id=1, source_target_pairs={{0,4},{1,11},{2,6},{3,9},{4,0},{5,15},{6,2},{7,13},{8,12},{9,3},{1... | collective-permute-start | bytes 258056 | tf_op jit(solution)/shard_map/ppermute | solution.py:22
  44.2 5.4 %collective-permute-start.17 = (bf16[24,1792]{1,0:T(8,128)(2,1)S(1)}, bf16[24,1792]{1,0:T(8,128)(2,1)S(1)}, u32[]{:S(2)}, u32[]{:S(2)}) collective-permute-start(bf16[24,1792]{1,0:T(8,128)(2,1)S(1)} %get-tuple-element.42), channel_id=1, source_target_pairs={{0,6},{1,9},{2,4},{3,11},{4,2},{5,13},{6,0},{7,15},{8,14},{9,1},{1... | collective-permute-start | bytes 258056 | tf_op jit(solution)/shard_map/ppermute | solution.py:22
  45.8 4.0 %collective-permute-start.21 = (bf16[24,896]{1,0:T(8,128)(2,1)S(1)}, bf16[24,896]{1,0:T(8,128)(2,1)S(1)}, u32[]{:S(2)}, u32[]{:S(2)}) collective-permute-start(bf16[24,896]{1,0:T(8,128)(2,1)S(1)} %get-tuple-element.48), channel_id=1, source_target_pairs={{0,1},{1,0},{2,3},{3,2},{4,5},{5,4},{6,7},{7,6},{8,9},{9,8},{10,11... | collective-permute-start | bytes 129032 | tf_op jit(solution)/shard_map/ppermute | solution.py:22
  49.7 2.1 %collective-permute-start.18 = (bf16[24,896]{1,0:T(8,128)(2,1)S(1)}, bf16[24,896]{1,0:T(8,128)(2,1)S(1)}, u32[]{:S(2)}, u32[]{:S(2)}) collective-permute-start(bf16[24,896]{1,0:T(8,128)(2,1)S(1)} %get-tuple-element.44), channel_id=1, source_target_pairs={{0,1},{1,0},{2,3},{3,2},{4,5},{5,4},{6,7},{7,6},{8,9},{9,8},{10,11... | collective-permute-start | bytes 129032 | tf_op jit(solution)/shard_map/ppermute | solution.py:22
  49.8 5.0 %collective-permute-start.22 = (bf16[24,896]{1,0:T(8,128)(2,1)S(1)}, bf16[24,896]{1,0:T(8,128)(2,1)S(1)}, u32[]{:S(2)}, u32[]{:S(2)}) collective-permute-start(bf16[24,896]{1,0:T(8,128)(2,1)S(1)} %shard_map.91), channel_id=1, source_target_pairs={{0,16},{1,17},{2,18},{3,19},{4,20},{5,21},{6,22},{7,23},{8,24},{9,... | collective-permute-start | bytes 129032 | tf_op jit(solution)/shard_map/ppermute | solution.py:22

commit v4 on v3

--- a/solution.py
+++ b/solution.py
@@ -13,6 +13,7 @@
 ANY = pl.BlockSpec(memory_space=pl.ANY)
 HBM = pl.BlockSpec(memory_space=pltpu.HBM)
 PARTS = 4
+LOADS = 4
 MIB = 1024 * 1024
 
 
@@ -102,9 +103,17 @@
     count = (len(refs) - 2) // 2
     token_ref, sems = refs[-2:]
     token_ref[...] = jnp.zeros_like(token_ref)
-    copies = [
-        pltpu.make_async_copy(refs[i], refs[count + i], sems.at[i]) for i in range(count)
-    ]
+    copies = []
+    for i in range(count):
+        source, target = refs[i], refs[count + i]
+        step = source.shape[1] // LOADS
+        for j in range(LOADS):
+            piece = pl.ds(j * step, step)
+            copies.append(
+                pltpu.make_async_copy(
+                    source.at[:, piece], target.at[:, piece], sems.at[i * LOADS + j]
+                )
+            )
     for copy in copies:
         copy.start()
     for copy in copies:
@@ -281,15 +290,20 @@
     moved = swapped(packed, far)
     beside = swapped(packed, 1)
     weights = [pltpu.with_memory_space_constraint(w, pltpu.HBM) for w in (w_gate, w_up, w_down)]
-    *loaded, token = call(
-        load_kernel,
-        [pltpu.VMEM(w.shape, w.dtype) for w in weights] + [shape((8, 128), f32)],
-        MIB,
-        *weights,
-        specs=[HBM] * 3,
-        scratch=[pltpu.SemaphoreType.DMA((3,))],
-    )
-    loaded = [pltpu.with_memory_space_constraint(w, pltpu.VMEM) for w in loaded]
+
+    def load(*arrays):
+        *loaded, token = call(
+            load_kernel,
+            [pltpu.VMEM(w.shape, w.dtype) for w in arrays] + [shape((8, 128), f32)],
+            MIB,
+            *arrays,
+            specs=[HBM] * len(arrays),
+            scratch=[pltpu.SemaphoreType.DMA((len(arrays) * LOADS,))],
+        )
+        return [pltpu.with_memory_space_constraint(w, pltpu.VMEM) for w in loaded], token
+
+    loaded, token = load(*weights[:2])
+    loaded = [*loaded, *load(weights[2])[0]]
     rows = 4 * tokens
     block, side = call(
         combine_kernel,

time: 55.6 us -> 54.5 us (0.980)
  waiting for transfers between devices: 22.4 us -> 19.7 us
  Pallas kernels: 10.3 us -> 11.9 us
    ppermute x23, waiting for transfers between devices: 22.4 us -> 19.7 us  [swapped(): return lax.ppermute(array, 'ep', pairs)]
    pallas_call x11 -> x12, Pallas kernels: 10.3 us -> 11.9 us  [call(): pl.pallas_call(kernel, out_shape=outs[0] if single else tuple(outs), in_s...]
  transfers between devices with their start and end apart: 23 -> 23, of which waited for: 10 -> 10; matrix products, arithmetic and copies ran while one was open for 0% -> 0% of each run, Pallas kernels for 15% -> 19%
where the time goes in v4:
time: 54.5 us; the launch traced here: 54.4 us
  starting transfers between devices  22.6 us (41%)
  waiting for transfers between devices  19.7 us (36%)
  Pallas kernels  11.9 us (22%)
    ppermute x23, starting transfers between devices, swapped(): return lax.ppermute(array, 'ep', pairs)  22.6 us
    ppermute x23, waiting for transfers between devices, swapped(): return lax.ppermute(array, 'ep', pairs)  19.7 us
    pallas_call x12, Pallas kernels, call(): pl.pallas_call(kernel, out_shape=outs[0] if single else tuple(outs), in_s...  11.9 us
  transfers between devices with their start and end apart: 23, of which 10 were waited for; matrix products, arithmetic and copies ran while one was open for 0% of the time, Pallas kernels for 19%

profile of v4, /device:TPU:0, one launch (start us, length us, event | category | flops | bytes accessed | tf_op | source)
XLA Modules:
  0.0 54.4 jit_solution(11963678629011906916)
XLA Ops:
  0.0 1.1 %shard_map.82.own_ref = bf16[24,1024]{1,0:T(8,128)(2,1)S(1)} custom-call(s32[2]{0:T(128)} %draft_hbm.1, bf16[6,3584]{1,0:T(8,128)(2,1)} %states_hbm.1, f32[3584]{0:T(1024)} %gain_hbm.1, f32[6,8]{1,0:T(8,128)} %scores_hbm.1, s32[6,8]{1,0:T(8,128)} %routes_hbm.1), custom_call_target="tpu_custom_call" | custom-call | bytes 106888 | tf_op jit(solution)/shard_map/pallas_call | solution.py:46
  1.1 4.1 %collective-permute-start.1 = (bf16[24,1024]{1,0:T(8,128)(2,1)S(1)}, bf16[24,1024]{1,0:T(8,128)(2,1)S(1)}, u32[]{:S(2)}, u32[]{:S(2)}) collective-permute-start(bf16[24,1024]{1,0:T(8,128)(2,1)S(1)} %shard_map.82.own_ref), channel_id=1, source_target_pairs={{0,16},{1,17},{2,18},{3,19},{4,20},{5,21},{6,22},{7,23},{8,24},{9,... | collective-permute-start | bytes 147464 | tf_op jit(solution)/shard_map/ppermute | solution.py:23
  5.2 2.6 %collective-permute-done.1.far_ref = bf16[24,1024]{1,0:T(8,128)(2,1)S(1)} collective-permute-done((bf16[24,1024]{1,0:T(8,128)(2,1)S(1)}, bf16[24,1024]{1,0:T(8,128)(2,1)S(1)}, u32[]{:S(2)}, u32[]{:S(2)}) %collective-permute-start.1) | collective-permute-done | bytes 49184 | tf_op jit(solution)/shard_map/ppermute | solution.py:23
  7.8 3.2 %shard_map.83 = (bf16[1,3584,512]{2,1,0:T(8,128)(2,1)S(1)}, bf16[1,3584,512]{2,1,0:T(8,128)(2,1)S(1)}, f32[8,128]{1,0:T(8,128)S(1)}) custom-call(bf16[1,3584,512]{2,1,0:T(8,128)(2,1)} %refs_0_.2, bf16[1,3584,512]{2,1,0:T(8,128)(2,1)} %refs_1_.1), custom_call_target="tpu_custom_call" | custom-call | bytes 14684160 | tf_op jit(solution)/shard_map/pallas_call | solution.py:46
  11.1 1.8 %collective-permute-start.11 = (bf16[24,3840]{1,0:T(8,128)(2,1)S(1)}, bf16[24,3840]{1,0:T(8,128)(2,1)S(1)}, u32[]{:S(2)}, u32[]{:S(2)}) collective-permute-start(bf16[24,3840]{1,0:T(8,128)(2,1)S(1)} %get-tuple-element.28.refs_0_), channel_id=1, source_target_pairs={{0,4},{1,11},{2,6},{3,9},{4,0},{5,15},{6,2},{7,13},{8,12},{9,3},{1... | collective-permute-start | bytes 552968 | tf_op jit(solution)/shard_map/ppermute | solution.py:23
  12.9 1.4 %collective-permute-start.12 = (bf16[24,3840]{1,0:T(8,128)(2,1)S(1)}, bf16[24,3840]{1,0:T(8,128)(2,1)S(1)}, u32[]{:S(2)}, u32[]{:S(2)}) collective-permute-start(bf16[24,3840]{1,0:T(8,128)(2,1)S(1)} %get-tuple-element.28.refs_0_), channel_id=1, source_target_pairs={{0,6},{1,9},{2,4},{3,11},{4,2},{5,13},{6,0},{7,15},{8,14},{9,1},{1... | collective-permute-start | bytes 552968 | tf_op jit(solution)/shard_map/ppermute | solution.py:23
  14.7 2.0 %collective-permute-done.11.refs_0_ = bf16[24,3840]{1,0:T(8,128)(2,1)S(1)} collective-permute-done((bf16[24,3840]{1,0:T(8,128)(2,1)S(1)}, bf16[24,3840]{1,0:T(8,128)(2,1)S(1)}, u32[]{:S(2)}, u32[]{:S(2)}) %collective-permute-start.11) | collective-permute-done | bytes 184352 | tf_op jit(solution)/shard_map/ppermute | solution.py:23
  17.1 3.2 %collective-permute-done.12.refs_1_ = bf16[24,3840]{1,0:T(8,128)(2,1)S(1)} collective-permute-done((bf16[24,3840]{1,0:T(8,128)(2,1)S(1)}, bf16[24,3840]{1,0:T(8,128)(2,1)S(1)}, u32[]{:S(2)}, u32[]{:S(2)}) %collective-permute-start.12) | collective-permute-done | bytes 184352 | tf_op jit(solution)/shard_map/ppermute | solution.py:23
  20.3 3.0 %collective-permute-start.5 = (bf16[24,1920]{1,0:T(8,128)(2,1)S(1)}, bf16[24,1920]{1,0:T(8,128)(2,1)S(1)}, u32[]{:S(2)}, u32[]{:S(2)}) collective-permute-start(bf16[24,1920]{1,0:T(8,128)(2,1)S(1)} %get-tuple-element.29), channel_id=1, source_target_pairs={{0,14},{1,15},{2,12},{3,13},{4,10},{5,11},{6,8},{7,9},{8,6},{9,7},... | collective-permute-start | bytes 276488 | tf_op jit(solution)/shard_map/ppermute | solution.py:23
  23.5 2.6 %shard_map.85 = (bf16[1,512,3584]{2,1,0:T(8,128)(2,1)S(1)}, f32[8,128]{1,0:T(8,128)}) custom-call(bf16[1,512,3584]{2,1,0:T(8,128)(2,1)} %refs_0_.3), custom_call_target="tpu_custom_call" | custom-call | bytes 7344128 | tf_op jit(solution)/shard_map/pallas_call | solution.py:46
  26.1 1.0 %collective-permute-done.5.refs_3_ = bf16[24,1920]{1,0:T(8,128)(2,1)S(1)} collective-permute-done((bf16[24,1920]{1,0:T(8,128)(2,1)S(1)}, bf16[24,1920]{1,0:T(8,128)(2,1)S(1)}, u32[]{:S(2)}, u32[]{:S(2)}) %collective-permute-start.5) | collective-permute-done | bytes 92192 | tf_op jit(solution)/shard_map/ppermute | solution.py:23
  27.2 2.0 %shard_map.88 = (f32[48,3584]{1,0:T(8,128)S(1)}, bf16[48,3584]{1,0:T(8,128)(2,1)S(1)}) custom-call(bf16[24,3840]{1,0:T(8,128)(2,1)S(1)} %collective-permute-done.11.refs_0_, bf16[24,3840]{1,0:T(8,128)(2,1)S(1)} %collective-permute-done.12.refs_1_, bf16[24,3840]{1,0:T(8,128)(2,1)S(1)} %collective-permute-done.13.refs_2_, ...), custom_call_target="tpu_custom_call" | custom-call | flops 1056964608 | bytes 12779520 | tf_op jit(solution)/shard_map/pallas_call | solution.py:46
  29.7 1.9 %shard_map.86 = (f32[48,3584]{1,0:T(8,128)S(1)}, bf16[24,3584]{1,0:T(8,128)(2,1)S(1)}, f32[24,1792]{1,0:T(8,128)S(1)}, bf16[24,1792]{1,0:T(8,128)(2,1)S(1)}) custom-call(bf16[24,3840]{1,0:T(8,128)(2,1)S(1)} %get-tuple-element.28.refs_0_, bf16[24,3840]{1,0:T(8,128)(2,1)S(1)} %collective-permute-done.3.refs_1_, ...), custom_call_target="tpu_custom_call" | custom-call | flops 1056964608 | bytes 12865536 | tf_op jit(solution)/shard_map/pallas_call | solution.py:46
  32.2 1.0 %collective-permute-done.8.refs_3_ = bf16[24,1792]{1,0:T(8,128)(2,1)S(1)} collective-permute-done((bf16[24,1792]{1,0:T(8,128)(2,1)S(1)}, bf16[24,1792]{1,0:T(8,128)(2,1)S(1)}, u32[]{:S(2)}, u32[]{:S(2)}) %collective-permute-start.8) | collective-permute-done | bytes 86048 | tf_op jit(solution)/shard_map/ppermute | solution.py:23
  33.3 2.5 %collective-permute-start.10 = (bf16[24,3584]{1,0:T(8,128)(2,1)S(1)}, bf16[24,3584]{1,0:T(8,128)(2,1)S(1)}, u32[]{:S(2)}, u32[]{:S(2)}) collective-permute-start(bf16[24,3584]{1,0:T(8,128)(2,1)S(1)} %get-tuple-element.38), channel_id=1, source_target_pairs={{0,2},{1,13},{2,0},{3,15},{4,6},{5,9},{6,4},{7,11},{8,10},{9,5},{1... | collective-permute-start | bytes 516104 | tf_op jit(solution)/shard_map/ppermute | solution.py:23
  36.5 1.6 %collective-permute-start.19 = (bf16[24,1792]{1,0:T(8,128)(2,1)S(1)}, bf16[24,1792]{1,0:T(8,128)(2,1)S(1)}, u32[]{:S(2)}, u32[]{:S(2)}) collective-permute-start(bf16[24,1792]{1,0:T(8,128)(2,1)S(1)} %get-tuple-element.45), channel_id=1, source_target_pairs={{0,4},{1,11},{2,6},{3,9},{4,0},{5,15},{6,2},{7,13},{8,12},{9,3},{1... | collective-permute-start | bytes 258056 | tf_op jit(solution)/shard_map/ppermute | solution.py:23
  38.1 1.9 %collective-permute-start.20 = (bf16[24,1792]{1,0:T(8,128)(2,1)S(1)}, bf16[24,1792]{1,0:T(8,128)(2,1)S(1)}, u32[]{:S(2)}, u32[]{:S(2)}) collective-permute-start(bf16[24,1792]{1,0:T(8,128)(2,1)S(1)} %get-tuple-element.46), channel_id=1, source_target_pairs={{0,6},{1,9},{2,4},{3,11},{4,2},{5,13},{6,0},{7,15},{8,14},{9,1},{1... | collective-permute-start | bytes 258056 | tf_op jit(solution)/shard_map/ppermute | solution.py:23
  40.0 1.5 %collective-permute-start.16 = (bf16[24,1792]{1,0:T(8,128)(2,1)S(1)}, bf16[24,1792]{1,0:T(8,128)(2,1)S(1)}, u32[]{:S(2)}, u32[]{:S(2)}) collective-permute-start(bf16[24,1792]{1,0:T(8,128)(2,1)S(1)} %get-tuple-element.41), channel_id=1, source_target_pairs={{0,4},{1,11},{2,6},{3,9},{4,0},{5,15},{6,2},{7,13},{8,12},{9,3},{1... | collective-permute-start | bytes 258056 | tf_op jit(solution)/shard_map/ppermute | solution.py:23
  41.5 1.6 %collective-permute-done.9.refs_1_ = bf16[24,1792]{1,0:T(8,128)(2,1)S(1)} collective-permute-done((bf16[24,1792]{1,0:T(8,128)(2,1)S(1)}, bf16[24,1792]{1,0:T(8,128)(2,1)S(1)}, u32[]{:S(2)}, u32[]{:S(2)}) %collective-permute-start.9) | collective-permute-done | bytes 86048 | tf_op jit(solution)/shard_map/ppermute | solution.py:23
  43.1 1.5 %collective-permute-done.20.refs_4_ = bf16[24,1792]{1,0:T(8,128)(2,1)S(1)} collective-permute-done((bf16[24,1792]{1,0:T(8,128)(2,1)S(1)}, bf16[24,1792]{1,0:T(8,128)(2,1)S(1)}, u32[]{:S(2)}, u32[]{:S(2)}) %collective-permute-start.20) | collective-permute-done | bytes 86048 | tf_op jit(solution)/shard_map/ppermute | solution.py:23
  45.3 3.2 %collective-permute-done.17.refs_4_ = bf16[24,1792]{1,0:T(8,128)(2,1)S(1)} collective-permute-done((bf16[24,1792]{1,0:T(8,128)(2,1)S(1)}, bf16[24,1792]{1,0:T(8,128)(2,1)S(1)}, u32[]{:S(2)}, u32[]{:S(2)}) %collective-permute-start.17) | collective-permute-done | bytes 86048 | tf_op jit(solution)/shard_map/ppermute | solution.py:23
  48.7 2.0 %collective-permute-start.22 = (bf16[24,896]{1,0:T(8,128)(2,1)S(1)}, bf16[24,896]{1,0:T(8,128)(2,1)S(1)}, u32[]{:S(2)}, u32[]{:S(2)}) collective-permute-start(bf16[24,896]{1,0:T(8,128)(2,1)S(1)} %shard_map.92), channel_id=1, source_target_pairs={{0,16},{1,17},{2,18},{3,19},{4,20},{5,21},{6,22},{7,23},{8,24},{9,... | collective-permute-start | bytes 129032 | tf_op jit(solution)/shard_map/ppermute | solution.py:23
  50.7 3.0 %collective-permute-done.22.other_ref = bf16[24,896]{1,0:T(8,128)(2,1)S(1)} collective-permute-done((bf16[24,896]{1,0:T(8,128)(2,1)S(1)}, bf16[24,896]{1,0:T(8,128)(2,1)S(1)}, u32[]{:S(2)}, u32[]{:S(2)}) %collective-permute-start.22) | collective-permute-done | bytes 43040 | tf_op jit(solution)/shard_map/ppermute | solution.py:23
  53.7 0.6 %shard_map.93 = bf16[6,3584]{1,0:T(8,128)(2,1)} custom-call(f32[24,896]{1,0:T(8,128)S(1)} %get-tuple-element.43.near_ref, bf16[24,896]{1,0:T(8,128)(2,1)S(1)} %collective-permute-done.18.beside_ref, bf16[24,896]{1,0:T(8,128)(2,1)S(1)} %collective-permute-done.22.other_ref), custom_call_target="tpu_custom_call" | custom-call | bytes 215040 | tf_op jit(solution)/shard_map/pallas_call | solution.py:46
  (34 shorter events, 3.9 us)
Async XLA Ops:
  1.1 6.7 %collective-permute-start.1 = (bf16[24,1024]{1,0:T(8,128)(2,1)S(1)}, bf16[24,1024]{1,0:T(8,128)(2,1)S(1)}, u32[]{:S(2)}, u32[]{:S(2)}) collective-permute-start(bf16[24,1024]{1,0:T(8,128)(2,1)S(1)} %shard_map.82.own_ref), channel_id=1, source_target_pairs={{0,16},{1,17},{2,18},{3,19},{4,20},{5,21},{6,22},{7,23},{8,24},{9,... | collective-permute-start | bytes 147464 | tf_op jit(solution)/shard_map/ppermute | solution.py:23
  5.2 5.8 %collective-permute-start = (bf16[24,1024]{1,0:T(8,128)(2,1)S(1)}, bf16[24,1024]{1,0:T(8,128)(2,1)S(1)}, u32[]{:S(2)}, u32[]{:S(2)}) collective-permute-start(bf16[24,1024]{1,0:T(8,128)(2,1)S(1)} %shard_map.82.own_ref), channel_id=1, source_target_pairs={{0,1},{1,0},{2,3},{3,2},{4,5},{5,4},{6,7},{7,6},{8,9},{9,8},{10,11... | collective-permute-start | bytes 147464 | tf_op jit(solution)/shard_map/ppermute | solution.py:23
  7.8 3.2 %collective-permute-start.2 = (bf16[24,1024]{1,0:T(8,128)(2,1)S(1)}, bf16[24,1024]{1,0:T(8,128)(2,1)S(1)}, u32[]{:S(2)}, u32[]{:S(2)}) collective-permute-start(bf16[24,1024]{1,0:T(8,128)(2,1)S(1)} %collective-permute-done.1.far_ref), channel_id=1, source_target_pairs={{0,1},{1,0},{2,3},{3,2},{4,5},{5,4},{6,7},{7,6},{8,9},{9,8},{10,11... | collective-permute-start | bytes 147464 | tf_op jit(solution)/shard_map/ppermute | solution.py:23
  11.1 5.6 %collective-permute-start.11 = (bf16[24,3840]{1,0:T(8,128)(2,1)S(1)}, bf16[24,3840]{1,0:T(8,128)(2,1)S(1)}, u32[]{:S(2)}, u32[]{:S(2)}) collective-permute-start(bf16[24,3840]{1,0:T(8,128)(2,1)S(1)} %get-tuple-element.28.refs_0_), channel_id=1, source_target_pairs={{0,4},{1,11},{2,6},{3,9},{4,0},{5,15},{6,2},{7,13},{8,12},{9,3},{1... | collective-permute-start | bytes 552968 | tf_op jit(solution)/shard_map/ppermute | solution.py:23
  12.9 7.4 %collective-permute-start.12 = (bf16[24,3840]{1,0:T(8,128)(2,1)S(1)}, bf16[24,3840]{1,0:T(8,128)(2,1)S(1)}, u32[]{:S(2)}, u32[]{:S(2)}) collective-permute-start(bf16[24,3840]{1,0:T(8,128)(2,1)S(1)} %get-tuple-element.28.refs_0_), channel_id=1, source_target_pairs={{0,6},{1,9},{2,4},{3,11},{4,2},{5,13},{6,0},{7,15},{8,14},{9,1},{1... | collective-permute-start | bytes 552968 | tf_op jit(solution)/shard_map/ppermute | solution.py:23
  14.3 8.9 %collective-permute-start.3 = (bf16[24,3840]{1,0:T(8,128)(2,1)S(1)}, bf16[24,3840]{1,0:T(8,128)(2,1)S(1)}, u32[]{:S(2)}, u32[]{:S(2)}) collective-permute-start(bf16[24,3840]{1,0:T(8,128)(2,1)S(1)} %get-tuple-element.28.refs_0_), channel_id=1, source_target_pairs={{0,2},{1,13},{2,0},{3,15},{4,6},{5,9},{6,4},{7,11},{8,10},{9,5},{1... | collective-permute-start | bytes 552968 | tf_op jit(solution)/shard_map/ppermute | solution.py:23
  16.7 10.5 %collective-permute-start.13 = (bf16[24,3840]{1,0:T(8,128)(2,1)S(1)}, bf16[24,3840]{1,0:T(8,128)(2,1)S(1)}, u32[]{:S(2)}, u32[]{:S(2)}) collective-permute-start(bf16[24,3840]{1,0:T(8,128)(2,1)S(1)} %collective-permute-done.11.refs_0_), channel_id=1, source_target_pairs={{0,1},{1,0},{2,3},{3,2},{4,5},{5,4},{6,7},{7,6},{8,9},{9,8},{10,11... | collective-permute-start | bytes 552968 | tf_op jit(solution)/shard_map/ppermute | solution.py:23
  20.3 6.9 %collective-permute-start.14 = (bf16[24,3840]{1,0:T(8,128)(2,1)S(1)}, bf16[24,3840]{1,0:T(8,128)(2,1)S(1)}, u32[]{:S(2)}, u32[]{:S(2)}) collective-permute-start(bf16[24,3840]{1,0:T(8,128)(2,1)S(1)} %collective-permute-done.12.refs_1_), channel_id=1, source_target_pairs={{0,1},{1,0},{2,3},{3,2},{4,5},{5,4},{6,7},{7,6},{8,9},{9,8},{10,11... | collective-permute-start | bytes 552968 | tf_op jit(solution)/shard_map/ppermute | solution.py:23
  20.3 6.9 %collective-permute-start.5 = (bf16[24,1920]{1,0:T(8,128)(2,1)S(1)}, bf16[24,1920]{1,0:T(8,128)(2,1)S(1)}, u32[]{:S(2)}, u32[]{:S(2)}) collective-permute-start(bf16[24,1920]{1,0:T(8,128)(2,1)S(1)} %get-tuple-element.29), channel_id=1, source_target_pairs={{0,14},{1,15},{2,12},{3,13},{4,10},{5,11},{6,8},{7,9},{8,6},{9,7},... | collective-permute-start | bytes 276488 | tf_op jit(solution)/shard_map/ppermute | solution.py:23
  23.3 6.4 %collective-permute-start.4 = (bf16[24,3840]{1,0:T(8,128)(2,1)S(1)}, bf16[24,3840]{1,0:T(8,128)(2,1)S(1)}, u32[]{:S(2)}, u32[]{:S(2)}) collective-permute-start(bf16[24,3840]{1,0:T(8,128)(2,1)S(1)} %collective-permute-done.3.refs_1_), channel_id=1, source_target_pairs={{0,1},{1,0},{2,3},{3,2},{4,5},{5,4},{6,7},{7,6},{8,9},{9,8},{10,11... | collective-permute-start | bytes 552968 | tf_op jit(solution)/shard_map/ppermute | solution.py:23
  27.2 2.5 %collective-permute-start.6 = (bf16[24,1920]{1,0:T(8,128)(2,1)S(1)}, bf16[24,1920]{1,0:T(8,128)(2,1)S(1)}, u32[]{:S(2)}, u32[]{:S(2)}) collective-permute-start(bf16[24,1920]{1,0:T(8,128)(2,1)S(1)} %collective-permute-done.5.refs_3_), channel_id=1, source_target_pairs={{0,1},{1,0},{2,3},{3,2},{4,5},{5,4},{6,7},{7,6},{8,9},{9,8},{10,11... | collective-permute-start | bytes 276488 | tf_op jit(solution)/shard_map/ppermute | solution.py:23
  29.1 7.3 %collective-permute-start.15 = (bf16[48,3584]{1,0:T(8,128)(2,1)S(1)}, bf16[48,3584]{1,0:T(8,128)(2,1)S(1)}, u32[]{:S(2)}, u32[]{:S(2)}) collective-permute-start(bf16[48,3584]{1,0:T(8,128)(2,1)S(1)} %get-tuple-element.40), channel_id=1, source_target_pairs={{0,1},{1,0},{2,3},{3,2},{4,5},{5,4},{6,7},{7,6},{8,9},{9,8},{10,11... | collective-permute-start | bytes 1032200 | tf_op jit(solution)/shard_map/ppermute | solution.py:23
  31.7 1.6 %collective-permute-start.7 = (bf16[24,3584]{1,0:T(8,128)(2,1)S(1)}, bf16[24,3584]{1,0:T(8,128)(2,1)S(1)}, u32[]{:S(2)}, u32[]{:S(2)}) collective-permute-start(bf16[24,3584]{1,0:T(8,128)(2,1)S(1)} %get-tuple-element.34), channel_id=1, source_target_pairs={{0,1},{1,0},{2,3},{3,2},{4,5},{5,4},{6,7},{7,6},{8,9},{9,8},{10,11... | collective-permute-start | bytes 516104 | tf_op jit(solution)/shard_map/ppermute | solution.py:23
  31.8 1.5 %collective-permute-start.8 = (bf16[24,1792]{1,0:T(8,128)(2,1)S(1)}, bf16[24,1792]{1,0:T(8,128)(2,1)S(1)}, u32[]{:S(2)}, u32[]{:S(2)}) collective-permute-start(bf16[24,1792]{1,0:T(8,128)(2,1)S(1)} %get-tuple-element.36), channel_id=1, source_target_pairs={{0,1},{1,0},{2,3},{3,2},{4,5},{5,4},{6,7},{7,6},{8,9},{9,8},{10,11... | collective-permute-start | bytes 258056 | tf_op jit(solution)/shard_map/ppermute | solution.py:23
  33.3 9.8 %collective-permute-start.10 = (bf16[24,3584]{1,0:T(8,128)(2,1)S(1)}, bf16[24,3584]{1,0:T(8,128)(2,1)S(1)}, u32[]{:S(2)}, u32[]{:S(2)}) collective-permute-start(bf16[24,3584]{1,0:T(8,128)(2,1)S(1)} %get-tuple-element.38), channel_id=1, source_target_pairs={{0,2},{1,13},{2,0},{3,15},{4,6},{5,9},{6,4},{7,11},{8,10},{9,5},{1... | collective-permute-start | bytes 516104 | tf_op jit(solution)/shard_map/ppermute | solution.py:23
  35.8 7.3 %collective-permute-start.9 = (bf16[24,1792]{1,0:T(8,128)(2,1)S(1)}, bf16[24,1792]{1,0:T(8,128)(2,1)S(1)}, u32[]{:S(2)}, u32[]{:S(2)}) collective-permute-start(bf16[24,1792]{1,0:T(8,128)(2,1)S(1)} %get-tuple-element.37), channel_id=1, source_target_pairs={{0,14},{1,15},{2,12},{3,13},{4,10},{5,11},{6,8},{7,9},{8,6},{9,7},... | collective-permute-start | bytes 258056 | tf_op jit(solution)/shard_map/ppermute | solution.py:23
  36.5 6.6 %collective-permute-start.19 = (bf16[24,1792]{1,0:T(8,128)(2,1)S(1)}, bf16[24,1792]{1,0:T(8,128)(2,1)S(1)}, u32[]{:S(2)}, u32[]{:S(2)}) collective-permute-start(bf16[24,1792]{1,0:T(8,128)(2,1)S(1)} %get-tuple-element.45), channel_id=1, source_target_pairs={{0,4},{1,11},{2,6},{3,9},{4,0},{5,15},{6,2},{7,13},{8,12},{9,3},{1... | collective-permute-start | bytes 258056 | tf_op jit(solution)/shard_map/ppermute | solution.py:23
  38.1 6.5 %collective-permute-start.20 = (bf16[24,1792]{1,0:T(8,128)(2,1)S(1)}, bf16[24,1792]{1,0:T(8,128)(2,1)S(1)}, u32[]{:S(2)}, u32[]{:S(2)}) collective-permute-start(bf16[24,1792]{1,0:T(8,128)(2,1)S(1)} %get-tuple-element.46), channel_id=1, source_target_pairs={{0,6},{1,9},{2,4},{3,11},{4,2},{5,13},{6,0},{7,15},{8,14},{9,1},{1... | collective-permute-start | bytes 258056 | tf_op jit(solution)/shard_map/ppermute | solution.py:23
  40.0 5.3 %collective-permute-start.16 = (bf16[24,1792]{1,0:T(8,128)(2,1)S(1)}, bf16[24,1792]{1,0:T(8,128)(2,1)S(1)}, u32[]{:S(2)}, u32[]{:S(2)}) collective-permute-start(bf16[24,1792]{1,0:T(8,128)(2,1)S(1)} %get-tuple-element.41), channel_id=1, source_target_pairs={{0,4},{1,11},{2,6},{3,9},{4,0},{5,15},{6,2},{7,13},{8,12},{9,3},{1... | collective-permute-start | bytes 258056 | tf_op jit(solution)/shard_map/ppermute | solution.py:23
  43.1 5.4 %collective-permute-start.17 = (bf16[24,1792]{1,0:T(8,128)(2,1)S(1)}, bf16[24,1792]{1,0:T(8,128)(2,1)S(1)}, u32[]{:S(2)}, u32[]{:S(2)}) collective-permute-start(bf16[24,1792]{1,0:T(8,128)(2,1)S(1)} %get-tuple-element.42), channel_id=1, source_target_pairs={{0,6},{1,9},{2,4},{3,11},{4,2},{5,13},{6,0},{7,15},{8,14},{9,1},{1... | collective-permute-start | bytes 258056 | tf_op jit(solution)/shard_map/ppermute | solution.py:23
  44.7 4.0 %collective-permute-start.21 = (bf16[24,896]{1,0:T(8,128)(2,1)S(1)}, bf16[24,896]{1,0:T(8,128)(2,1)S(1)}, u32[]{:S(2)}, u32[]{:S(2)}) collective-permute-start(bf16[24,896]{1,0:T(8,128)(2,1)S(1)} %get-tuple-element.48), channel_id=1, source_target_pairs={{0,1},{1,0},{2,3},{3,2},{4,5},{5,4},{6,7},{7,6},{8,9},{9,8},{10,11... | collective-permute-start | bytes 129032 | tf_op jit(solution)/shard_map/ppermute | solution.py:23
  48.6 2.1 %collective-permute-start.18 = (bf16[24,896]{1,0:T(8,128)(2,1)S(1)}, bf16[24,896]{1,0:T(8,128)(2,1)S(1)}, u32[]{:S(2)}, u32[]{:S(2)}) collective-permute-start(bf16[24,896]{1,0:T(8,128)(2,1)S(1)} %get-tuple-element.44), channel_id=1, source_target_pairs={{0,1},{1,0},{2,3},{3,2},{4,5},{5,4},{6,7},{7,6},{8,9},{9,8},{10,11... | collective-permute-start | bytes 129032 | tf_op jit(solution)/shard_map/ppermute | solution.py:23
  48.7 5.0 %collective-permute-start.22 = (bf16[24,896]{1,0:T(8,128)(2,1)S(1)}, bf16[24,896]{1,0:T(8,128)(2,1)S(1)}, u32[]{:S(2)}, u32[]{:S(2)}) collective-permute-start(bf16[24,896]{1,0:T(8,128)(2,1)S(1)} %shard_map.92), channel_id=1, source_target_pairs={{0,16},{1,17},{2,18},{3,19},{4,20},{5,21},{6,22},{7,23},{8,24},{9,... | collective-permute-start | bytes 129032 | tf_op jit(solution)/shard_map/ppermute | solution.py:23
